TPU v7x, 32 devices: a whole 2x2x4 slice. The times are simulated.
32 devices in a mesh: groups: 1, row: 16 (over z, y, core), col: 2 (over x), rep: 1.
Axes of the slice: x: 2, y: 2, z: 4, core: 2. Of those that a mesh axis runs over, the one named last changes fastest.
Arguments:
- bins: bfloat16 [256, 1536], P(('groups', 'row', 'col')), may hold values from -6 to 6
- row_proj: bfloat16 [96, 1536], P('rep'), may hold values from -0.15625 to 0.15625
- col_proj: bfloat16 [96, 1536], P('rep'), may hold values from -0.15625 to 0.15625
- conv_weight: bfloat16 [3, 9, 96, 96], P(None, None, 'rep'), may hold values from -0.21875 to 0.21875
- conv_bias: float32 [3, 96], P(None, 'rep'), may hold values from -3 to 3
Outputs:
- contact_map: bfloat16 [96, 256, 256], P('rep', ('groups', 'row'), 'col')
All inputs are finite; a program needn't handle non-finite values.
Results may differ from a plain program's by a relative error of at most 0.013.
Values may be sent and summed in bfloat16 or wider, within the bound.
No kernel may reach another device: no remote copies, remote signals or barrier semaphores. Data moves between devices by JAX's collectives and lax.ppermute only.
A program may use at most 128 MiB of HBM per device.

v0:
```python
import jax
import jax.numpy as jnp
from jax import lax
from jax.sharding import PartitionSpec as P


def with_halo(value, sides, width):
    for axis, dim in sides:
        devices, length = (lax.axis_size(axis), value.shape[dim])
        up = [(i, (i + 1) % devices) for i in range(devices - 1)]
        down = [(j, i) for i, j in up]
        last = lax.slice_in_dim(value, length - width, length, axis=dim)
        leading = lax.slice_in_dim(value, 0, width, axis=dim)
        before = lax.ppermute(last, axis, up)
        after = lax.ppermute(leading, axis, down)
        value = jnp.concatenate([before, value, after], axis=dim)
    return value


def conv_valid(padded, filters, spread, height, breadth):
    total = None
    for tap in range(9):
        first = tap // 3 * spread
        second = tap % 3 * spread
        window = padded[:, first : first + height, second : second + breadth]
        term = jnp.einsum("oi,ipq->opq", filters[tap], window, preferred_element_type=jnp.float32)
        total = term if total is None else total + term
    return total


def layer_step(state, filters, bias_row, spread):
    active = jnp.maximum(state, 0)
    whole = lax.all_gather(active, "rep", axis=0, tiled=True)
    padded = with_halo(whole, (("row", 1), ("col", 2)), spread)
    height = state.shape[1]
    breadth = state.shape[2]
    conv = conv_valid(padded, filters, spread, height, breadth)
    return (state.astype(jnp.float32) + conv + bias_row[:, None, None]).astype(jnp.bfloat16)


def outer_terms(left_terms, right_terms):
    return (
        left_terms.T.astype(jnp.float32)[:, :, None] * right_terms.T.astype(jnp.float32)[:, None, :]
    ).astype(jnp.bfloat16)


def whole_terms(row_terms, col_terms):
    return (
        lax.all_gather(row_terms, "rep", axis=1, tiled=True),
        lax.all_gather(col_terms, "rep", axis=1, tiled=True),
    )


def whole_filters(conv_weight, conv_bias):
    return (
        lax.all_gather(
            conv_weight.astype(jnp.float32).astype(jnp.bfloat16), "rep", axis=2, tiled=True
        ).astype(jnp.float32),
        lax.all_gather(conv_bias.astype(jnp.bfloat16), "rep", axis=1, tiled=True).astype(
            conv_bias.dtype
        ),
    )


def project_bins(bins, weights):
    return lax.dot_general(
        bins, weights, (((1,), (1,)), ((), ())), preferred_element_type=jnp.float32
    ).astype(jnp.bfloat16)


def shards(bins, row_proj, col_proj, conv_weight, conv_bias):
    span = bins.shape[0]
    rows_count = lax.axis_size("row")
    cols_count = lax.axis_size("col")
    total_bins = span * rows_count * cols_count
    tile_rows = total_bins // rows_count
    tile_cols = total_bins // cols_count
    row_index = lax.axis_index("row")
    col_index = lax.axis_index("col")
    row_local = project_bins(bins, row_proj)
    col_local = project_bins(bins, col_proj)
    row_terms, col_terms = (
        lax.all_gather(row_local, ("row", "col"), axis=0, tiled=True),
        lax.all_gather(col_local, ("row", "col"), axis=0, tiled=True),
    )
    all_rows = None
    all_cols = None
    all_filters = None
    all_bias = None
    own_rows = lax.dynamic_slice_in_dim(row_terms, row_index * tile_rows, tile_rows, 0)
    own_cols = lax.dynamic_slice_in_dim(col_terms, col_index * tile_cols, tile_cols, 0)
    state = outer_terms(own_rows, own_cols)
    state = layer_step(state, conv_weight[0], conv_bias[0], 1)
    state = layer_step(state, conv_weight[1], conv_bias[1], 2)
    half = state.shape[0]
    all_rows, all_cols = whole_terms(row_terms, col_terms)
    wide_filters, all_bias = whole_filters(conv_weight, conv_bias)
    all_filters = wide_filters.astype(jnp.bfloat16)
    first_filters = all_filters[0]
    first_bias = all_bias[0]
    margin = 3
    padded_rows = jnp.pad(all_rows, ((margin, margin), (0, 0)))
    padded_cols = jnp.pad(all_cols, ((margin, margin), (0, 0)))
    mirror_rows = lax.dynamic_slice_in_dim(
        padded_rows, col_index * tile_cols, tile_cols + 2 * margin, 0
    )
    mirror_cols = lax.dynamic_slice_in_dim(
        padded_cols, row_index * tile_rows, tile_rows + 2 * margin, 0
    )
    seed_map = outer_terms(mirror_rows, mirror_cols)
    inner_height = tile_cols + 4
    inner_breadth = tile_rows + 4
    conv_first = conv_valid(jnp.maximum(seed_map, 0), first_filters, 1, inner_height, inner_breadth)
    first_map = seed_map[:, 1:-1, 1:-1].astype(jnp.float32) + conv_first + first_bias[:, None, None]
    row_place = col_index * tile_cols - 2 + lax.iota(jnp.int32, inner_height)
    col_place = row_index * tile_rows - 2 + lax.iota(jnp.int32, inner_breadth)
    row_inside = (row_place >= 0) & (row_place < total_bins)
    col_inside = (col_place >= 0) & (col_place < total_bins)
    inside = row_inside[:, None] & col_inside[None, :]
    first_map = jnp.where(inside[None], first_map, 0.0).astype(jnp.bfloat16)
    own_half = lax.dynamic_slice_in_dim(first_map, lax.axis_index("rep") * half, half, 0)
    conv_second = conv_valid(jnp.maximum(first_map, 0), conv_weight[1], 2, tile_cols, tile_rows)
    second_map = (
        own_half[:, 2:-2, 2:-2].astype(jnp.float32) + conv_second + conv_bias[1][:, None, None]
    ).astype(jnp.bfloat16)
    mirror = second_map.transpose(0, 2, 1)
    state = ((state.astype(jnp.float32) + mirror.astype(jnp.float32)) * 0.5).astype(jnp.bfloat16)
    state = layer_step(state, conv_weight[2], conv_bias[2], 4)
    return state


def solution(mesh):
    placed = (
        P(("groups", "row", "col"), None),
        P("rep", None),
        P("rep", None),
        P(None, None, "rep", None),
        P(None, "rep"),
    )
    return jax.shard_map(
        shards,
        mesh=mesh,
        in_specs=placed,
        out_specs=P("rep", ("groups", "row"), "col"),
        check_vma=False,
    )
```

profile of v0, /device:TPU:0, one launch (start us, length us, event | category | flops | bytes accessed | tf_op | source)
XLA Modules:
  0.0 193.0 jit_solution(17881068901938080513)
XLA Ops:
  0.0 1.0 copy-done
  1.0 0.9 convolution_convert_fusion
  1.9 70.1 %all_gather.5 = bf16[256,96]{1,0:T(8,128)(2,1)S(1)} all-gather(bf16[8,96]{1,0:T(8,128)(2,1)S(1)} %convolution_convert_fusion), channel_id=1, replica_groups=mesh['groups'=1,'row'=16,'col'=2,'rep'=1] {'row','col'}, dimensions={0}, use_global_device_ids=true | all-gather | bytes 50688 | tf_op jit(solution)/shard_map/all_gather | solution.py:84
  71.9 1.1 convolution_convert_fusion.1
  73.1 63.7 %all_gather.4 = bf16[256,96]{1,0:T(8,128)(2,1)S(1)} all-gather(bf16[8,96]{1,0:T(8,128)(2,1)S(1)} %convolution_convert_fusion.1), channel_id=1, replica_groups=mesh['groups'=1,'row'=16,'col'=2,'rep'=1] {'row','col'}, dimensions={0}, use_global_device_ids=true | all-gather | bytes 50688 | tf_op jit(solution)/shard_map/all_gather | solution.py:83
  136.9 1.4 collective-permute-start
  138.4 1.3 collective-permute-start.1
  140.1 0.3 fusion.49
  140.4 0.3 convolution_add_fusion.7
  140.8 0.3 convolution_add_fusion.6
  141.1 0.4 convolution_add_fusion.5
  141.5 0.4 convolution_add_fusion.4
  141.8 0.4 convolution_add_fusion.3
  142.2 0.4 convolution_add_fusion.2
  142.6 0.4 convolution_add_fusion.1
  143.0 0.9 broadcast_maximum_fusion.1
  144.2 0.3 convolution_add_fusion.22
  144.5 0.3 convolution_add_fusion.21
  144.8 0.3 convolution_add_fusion.20
  145.1 0.3 convolution_add_fusion.19
  145.4 0.3 convolution_add_fusion.18
  145.8 0.3 convolution_add_fusion.17
  146.1 0.3 convolution_add_fusion.16
  146.4 0.4 fusion.39
  146.8 0.3 fusion.111
  147.2 4.2 %collective-permute-start.2 = (bf16[96,18,1]{0,2,1:T(2,128)(2,1)S(1)}, bf16[96,18,1]{0,2,1:T(2,128)(2,1)S(1)}, u32[]{:S(2)}, u32[]{:S(2)}) collective-permute-start(bf16[96,18,1]{0,2,1:T(2,128)(2,1)S(1)} %get-tuple-element.15), channel_id=1, source_target_pairs={{0,1},{2,3},{4,5},{6,7},{8,9},{10,11},{12,13},{14,15},{16,17},{18,... | collective-permute-start | bytes 10376 | tf_op jit(solution)/shard_map/ppermute | solution.py:14
  151.3 1.3 collective-permute-start.3
  152.6 0.3 fusion.66
  153.0 0.3 fusion.70
  153.3 3.6 %collective-permute-done.3 = bf16[96,18,1]{0,2,1:T(2,128)(2,1)S(1)} collective-permute-done((bf16[96,18,1]{0,2,1:T(2,128)(2,1)S(1)}, bf16[96,18,1]{0,2,1:T(2,128)(2,1)S(1)}, u32[]{:S(2)}, u32[]{:S(2)}) %collective-permute-start.3) | collective-permute-done | bytes 3488 | tf_op jit(solution)/shard_map/ppermute | solution.py:15
  157.2 0.3 fusion.108
  157.5 0.3 fusion.101
  158.4 0.4 fusion.28
  158.8 0.6 broadcast_maximum_fusion.3
  159.5 1.6 collective-permute-start.4
  161.1 1.3 collective-permute-start.5
  162.4 0.3 fusion.131
  162.7 1.5 collective-permute-done.5
  164.3 1.9 %collective-permute-start.6 = (bf16[96,20,2]{0,2,1:T(2,128)(2,1)S(1)}, bf16[96,20,2]{0,2,1:T(2,128)(2,1)S(1)}, u32[]{:S(2)}, u32[]{:S(2)}) collective-permute-start(bf16[96,20,2]{0,2,1:T(2,128)(2,1)S(1)} %get-tuple-element.11), channel_id=1, source_target_pairs={{0,1},{2,3},{4,5},{6,7},{8,9},{10,11},{12,13},{14,15},{16,17},{18,... | collective-permute-start | bytes 23048 | tf_op jit(solution)/shard_map/ppermute | solution.py:14
  166.2 1.5 collective-permute-start.7
  167.7 0.3 fusion.58
  168.0 0.3 fusion.62
  168.3 3.5 %collective-permute-done.7 = bf16[96,20,2]{0,2,1:T(2,128)(2,1)S(1)} collective-permute-done((bf16[96,20,2]{0,2,1:T(2,128)(2,1)S(1)}, bf16[96,20,2]{0,2,1:T(2,128)(2,1)S(1)}, u32[]{:S(2)}, u32[]{:S(2)}) %collective-permute-start.7) | collective-permute-done | bytes 7712 | tf_op jit(solution)/shard_map/ppermute | solution.py:15
  172.1 0.3 fusion.98
  172.4 0.3 fusion.91
  173.3 0.5 fusion.19
  173.8 0.6 broadcast_maximum_fusion.2
  174.4 2.9 %collective-permute-start.8 = (bf16[96,4,128]{0,2,1:T(8,128)(2,1)S(1)}, bf16[96,4,128]{0,2,1:T(8,128)(2,1)S(1)}, u32[]{:S(2)}, u32[]{:S(2)}) collective-permute-start(bf16[96,4,128]{0,2,1:T(8,128)(2,1)S(1)} %get-tuple-element.17), channel_id=1, source_target_pairs={{0,2},{2,4},{4,6},{6,8},{8,10},{10,12},{12,14},{14,16},{16,18},{18... | collective-permute-start | bytes 294920 | tf_op jit(solution)/shard_map/ppermute | solution.py:14
  177.4 1.3 collective-permute-start.9
  178.7 2.8 %collective-permute-done.9 = bf16[96,4,128]{0,2,1:T(8,128)(2,1)S(1)} collective-permute-done((bf16[96,4,128]{0,2,1:T(8,128)(2,1)S(1)}, bf16[96,4,128]{0,2,1:T(8,128)(2,1)S(1)}, u32[]{:S(2)}, u32[]{:S(2)}) %collective-permute-start.9) | collective-permute-done | bytes 98336 | tf_op jit(solution)/shard_map/ppermute | solution.py:15
  181.6 1.6 collective-permute-start.10
  183.2 1.3 collective-permute-start.11
  184.5 0.3 fusion.51
  184.9 4.1 %collective-permute-done.11 = bf16[96,24,4]{0,1,2:T(8,128)(2,1)S(1)} collective-permute-done((bf16[96,24,4]{0,1,2:T(8,128)(2,1)S(1)}, bf16[96,24,4]{0,1,2:T(8,128)(2,1)S(1)}, u32[]{:S(2)}, u32[]{:S(2)}) %collective-permute-start.11) | collective-permute-done | bytes 18464 | tf_op jit(solution)/shard_map/ppermute | solution.py:15
  188.9 0.3 maximum_maximum_fusion
  189.3 0.3 fusion.74
  189.6 0.3 convolution_add_fusion.14
  189.9 0.3 convolution_add_fusion.13
  190.2 0.3 convolution_add_fusion.12
  190.5 0.3 convolution_add_fusion.11
  190.9 0.3 convolution_add_fusion.10
  191.2 0.3 convolution_add_fusion.9
  191.5 0.4 fusion.36
  191.9 1.1 copy.128
  (42 shorter events, 2.8 us)
Async XLA Ops:
  0.0 1.0 copy-start
  136.8 3.3 %copy-start.2 = (f32[3,96]{1,0:T(4,128)S(1)}, f32[3,96]{1,0:T(4,128)}, u32[]{:S(2)}) copy-start(f32[3,96]{1,0:T(4,128)} %param.9) | copy-start | bytes 3460
  136.8 3.3 %copy-start.1 = (bf16[3,9,96,96]{3,2,1,0:T(8,128)(2,1)S(1)}, bf16[3,9,96,96]{3,2,1,0:T(8,128)(2,1)}, u32[]{:S(2)}) copy-start(bf16[3,9,96,96]{3,2,1,0:T(8,128)(2,1)} %param.8) | copy-start | bytes 1492996
  136.9 10.2 %collective-permute-start = (bf16[96,1,128]{0,2,1:T(8,128)(2,1)S(1)}, bf16[96,1,128]{0,2,1:T(8,128)(2,1)S(1)}, u32[]{:S(2)}, u32[]{:S(2)}) collective-permute-start(bf16[96,1,128]{0,2,1:T(8,128)(2,1)S(1)} %get-tuple-element.21), channel_id=1, source_target_pairs={{0,2},{2,4},{4,6},{6,8},{8,10},{10,12},{12,14},{14,16},{16,18},{18... | collective-permute-start | bytes 73736 | tf_op jit(solution)/shard_map/ppermute | solution.py:14
  138.4 8.7 %collective-permute-start.1 = (bf16[96,1,128]{0,2,1:T(8,128)(2,1)S(1)}, bf16[96,1,128]{0,2,1:T(8,128)(2,1)S(1)}, u32[]{:S(2)}, u32[]{:S(2)}) collective-permute-start(bf16[96,1,128]{0,2,1:T(8,128)(2,1)S(1)} %get-tuple-element.22), channel_id=1, source_target_pairs={{2,0},{4,2},{6,4},{8,6},{10,8},{12,10},{14,12},{16,14},{18,16},{20... | collective-permute-start | bytes 73736 | tf_op jit(solution)/shard_map/ppermute | solution.py:15
  147.2 6.1 %collective-permute-start.2 = (bf16[96,18,1]{0,2,1:T(2,128)(2,1)S(1)}, bf16[96,18,1]{0,2,1:T(2,128)(2,1)S(1)}, u32[]{:S(2)}, u32[]{:S(2)}) collective-permute-start(bf16[96,18,1]{0,2,1:T(2,128)(2,1)S(1)} %get-tuple-element.15), channel_id=1, source_target_pairs={{0,1},{2,3},{4,5},{6,7},{8,9},{10,11},{12,13},{14,15},{16,17},{18,... | collective-permute-start | bytes 10376 | tf_op jit(solution)/shard_map/ppermute | solution.py:14
  151.3 5.6 %collective-permute-start.3 = (bf16[96,18,1]{0,2,1:T(2,128)(2,1)S(1)}, bf16[96,18,1]{0,2,1:T(2,128)(2,1)S(1)}, u32[]{:S(2)}, u32[]{:S(2)}) collective-permute-start(bf16[96,18,1]{0,2,1:T(2,128)(2,1)S(1)} %get-tuple-element.16), channel_id=1, source_target_pairs={{1,0},{3,2},{5,4},{7,6},{9,8},{11,10},{13,12},{15,14},{17,16},{19,... | collective-permute-start | bytes 10376 | tf_op jit(solution)/shard_map/ppermute | solution.py:15
  159.5 3.2 %collective-permute-start.4 = (bf16[96,2,128]{0,2,1:T(8,128)(2,1)S(1)}, bf16[96,2,128]{0,2,1:T(8,128)(2,1)S(1)}, u32[]{:S(2)}, u32[]{:S(2)}) collective-permute-start(bf16[96,2,128]{0,2,1:T(8,128)(2,1)S(1)} %get-tuple-element.19), channel_id=1, source_target_pairs={{0,2},{2,4},{4,6},{6,8},{8,10},{10,12},{12,14},{14,16},{16,18},{18... | collective-permute-start | bytes 147464 | tf_op jit(solution)/shard_map/ppermute | solution.py:14
  161.1 3.1 %collective-permute-start.5 = (bf16[96,2,128]{0,2,1:T(8,128)(2,1)S(1)}, bf16[96,2,128]{0,2,1:T(8,128)(2,1)S(1)}, u32[]{:S(2)}, u32[]{:S(2)}) collective-permute-start(bf16[96,2,128]{0,2,1:T(8,128)(2,1)S(1)} %get-tuple-element.20), channel_id=1, source_target_pairs={{2,0},{4,2},{6,4},{8,6},{10,8},{12,10},{14,12},{16,14},{18,16},{20... | collective-permute-start | bytes 147464 | tf_op jit(solution)/shard_map/ppermute | solution.py:15
  164.3 4.1 %collective-permute-start.6 = (bf16[96,20,2]{0,2,1:T(2,128)(2,1)S(1)}, bf16[96,20,2]{0,2,1:T(2,128)(2,1)S(1)}, u32[]{:S(2)}, u32[]{:S(2)}) collective-permute-start(bf16[96,20,2]{0,2,1:T(2,128)(2,1)S(1)} %get-tuple-element.11), channel_id=1, source_target_pairs={{0,1},{2,3},{4,5},{6,7},{8,9},{10,11},{12,13},{14,15},{16,17},{18,... | collective-permute-start | bytes 23048 | tf_op jit(solution)/shard_map/ppermute | solution.py:14
  166.2 5.6 %collective-permute-start.7 = (bf16[96,20,2]{0,2,1:T(2,128)(2,1)S(1)}, bf16[96,20,2]{0,2,1:T(2,128)(2,1)S(1)}, u32[]{:S(2)}, u32[]{:S(2)}) collective-permute-start(bf16[96,20,2]{0,2,1:T(2,128)(2,1)S(1)} %get-tuple-element.12), channel_id=1, source_target_pairs={{1,0},{3,2},{5,4},{7,6},{9,8},{11,10},{13,12},{15,14},{17,16},{19,... | collective-permute-start | bytes 23048 | tf_op jit(solution)/shard_map/ppermute | solution.py:15
  174.4 4.2 %collective-permute-start.8 = (bf16[96,4,128]{0,2,1:T(8,128)(2,1)S(1)}, bf16[96,4,128]{0,2,1:T(8,128)(2,1)S(1)}, u32[]{:S(2)}, u32[]{:S(2)}) collective-permute-start(bf16[96,4,128]{0,2,1:T(8,128)(2,1)S(1)} %get-tuple-element.17), channel_id=1, source_target_pairs={{0,2},{2,4},{4,6},{6,8},{8,10},{10,12},{12,14},{14,16},{16,18},{18... | collective-permute-start | bytes 294920 | tf_op jit(solution)/shard_map/ppermute | solution.py:14
  177.4 4.1 %collective-permute-start.9 = (bf16[96,4,128]{0,2,1:T(8,128)(2,1)S(1)}, bf16[96,4,128]{0,2,1:T(8,128)(2,1)S(1)}, u32[]{:S(2)}, u32[]{:S(2)}) collective-permute-start(bf16[96,4,128]{0,2,1:T(8,128)(2,1)S(1)} %get-tuple-element.18), channel_id=1, source_target_pairs={{2,0},{4,2},{6,4},{8,6},{10,8},{12,10},{14,12},{16,14},{18,16},{20... | collective-permute-start | bytes 294920 | tf_op jit(solution)/shard_map/ppermute | solution.py:15
  181.6 3.3 %collective-permute-start.10 = (bf16[96,24,4]{0,1,2:T(8,128)(2,1)S(1)}, bf16[96,24,4]{0,1,2:T(8,128)(2,1)S(1)}, u32[]{:S(2)}, u32[]{:S(2)}) collective-permute-start(bf16[96,24,4]{0,1,2:T(8,128)(2,1)S(1)} %copy.106), channel_id=1, source_target_pairs={{0,1},{2,3},{4,5},{6,7},{8,9},{10,11},{12,13},{14,15},{16,17},{18,... | collective-permute-start | bytes 55304 | tf_op jit(solution)/shard_map/ppermute | solution.py:14
  183.2 5.7 %collective-permute-start.11 = (bf16[96,24,4]{0,1,2:T(8,128)(2,1)S(1)}, bf16[96,24,4]{0,1,2:T(8,128)(2,1)S(1)}, u32[]{:S(2)}, u32[]{:S(2)}) collective-permute-start(bf16[96,24,4]{0,1,2:T(8,128)(2,1)S(1)} %copy.112), channel_id=1, source_target_pairs={{1,0},{3,2},{5,4},{7,6},{9,8},{11,10},{13,12},{15,14},{17,16},{19,... | collective-permute-start | bytes 55304 | tf_op jit(solution)/shard_map/ppermute | solution.py:15
where the time goes:
time: 195 us; the launch traced here: 193 us
  blocking collectives  134 us (69%)
  starting transfers between devices  21.7 us (11%)
  matrix products  17.8 us (9%)
  waiting for transfers between devices  15.5 us (8%)
  local copies, waits for them, and re-layouts  2.12 us (1%)
    all_gather x1, blocking collectives, shards(): lax.all_gather(col_local, ('row', 'col'), axis=0, tiled=True)  70.1 us
    all_gather x1, blocking collectives, shards(): lax.all_gather(row_local, ('row', 'col'), axis=0, tiled=True)  63.7 us
    dot_general x45, matrix products, conv_valid(): jnp.einsum('oi,ipq->opq', filters[tap], window, preferred_element_type=jn...  15.7 us
    ppermute x6, waiting for transfers between devices, with_halo(): after = lax.ppermute(leading, axis, down)  15.5 us
    ppermute x6, starting transfers between devices, with_halo(): before = lax.ppermute(last, axis, up)  13.7 us
    ppermute x6, starting transfers between devices, with_halo(): after = lax.ppermute(leading, axis, down)  7.93 us
  transfers between devices with their start and end apart: 12, of which 5 were waited for; matrix products, arithmetic and copies ran while one was open for 5% of the time, Pallas kernels for 0%

commit v1 on v0

v1 whole, which is shorter than its diff:
```python
import functools
import jax
import jax.numpy as jnp
from jax import lax
from jax.experimental import pallas as pl
from jax.experimental.pallas import tpu as pltpu
from jax.sharding import PartitionSpec as P

LANES = 128
PAD = 16
NT = (((1,), (1,)), ((), ()))


def pick(count, most):
    return max(k for k in range(1, min(count, most) + 1) if count % k == 0)


def decoder_kernel(tr, tc, terms_ref, w_ref, bias_ref, out_ref,
                   rows_f, cols_f, vtab, utab, w0, w1, w2, h1, sym, acc):
    bins = terms_ref.shape[0]
    ch = w_ref.shape[2]
    wide = tc + 16
    span = tc + 8
    i0 = lax.axis_index("row") * tr
    j0 = lax.axis_index("col") * tc
    f32, bf16 = jnp.float32, jnp.bfloat16

    for tab, lo in ((rows_f, 0), (cols_f, LANES)):
        tab[0:PAD] = jnp.zeros((PAD, LANES), f32)
        tab[PAD + bins:] = jnp.zeros((PAD, LANES), f32)
        tab[PAD:PAD + bins] = terms_ref[:, lo:lo + LANES].astype(f32)

    w0[...] = jnp.zeros(w0.shape, bf16)
    w1[...] = jnp.zeros(w1.shape, bf16)
    w2[...] = jnp.zeros(w2.shape, bf16)
    for q in range(4):
        for b in range(3):
            at = (q * 3 + b) * LANES
            for p in range(2):
                a = q - p
                if 0 <= a < 3:
                    rows = slice(p * LANES, p * LANES + ch)
                    w0[0, rows, at:at + ch] = w_ref[0, 3 * a + b]
                    w0[1, rows, at:at + ch] = w_ref[0, 3 * b + a]
                    w1[rows, at:at + ch] = w_ref[1, 3 * a + b]
                    w1[rows, 12 * LANES + at:12 * LANES + at + ch] = w_ref[1, 3 * b + a]
                    w2[p * ch:(p + 1) * ch, at:at + ch] = w_ref[2, 3 * a + b]
    eye = (lax.broadcasted_iota(jnp.int32, (ch, LANES), 0)
           == lax.broadcasted_iota(jnp.int32, (ch, LANES), 1))
    unit = jnp.where(eye, 1.0, 0.0)
    for p in range(2):
        at = (12 + p) * LANES
        w2[p * ch:(p + 1) * ch, at:at + LANES] = unit.astype(bf16)
    bias0 = bias_ref[0:1, :]
    bias1 = bias_ref[1:2, :]
    bias2 = jnp.broadcast_to(
        jnp.sum(unit * bias_ref[2:3, :], axis=1, keepdims=True), (ch, LANES))

    for m, (utab_f, vtab_f) in enumerate(((rows_f, cols_f), (cols_f, rows_f))):
        for b in range(3):
            vtab[m, b] = vtab_f[pl.ds(j0 + PAD - 9 + b, wide), :].astype(bf16)
        for i in range(tr + 14):
            row = utab_f[pl.ds(i0 + PAD - 7 + i, 1), :]
            utab[m, i] = jnp.broadcast_to(row, (16, LANES)).astype(bf16)

    def outer(m, i, b):
        v = vtab[m, b].reshape(wide // 16, 16, LANES)
        return (v * utab[m, i][None]).reshape(wide, LANES)

    pairs0 = (tr + 12) // 2
    step0 = pick(pairs0, 7)
    for m in range(2):
        def first(c, _, m=m):
            base = c * step0
            lhs = jnp.concatenate([
                jnp.concatenate([
                    jnp.maximum(outer(m, 2 * (base + g) + q, b), 0)
                    for q in range(4) for b in range(3)], axis=1)
                for g in range(step0)], axis=0)
            y = lax.dot_general(lhs, w0[m], NT, preferred_element_type=f32)
            for g in range(step0):
                for p in range(2):
                    i = 2 * (base + g) + p
                    own = outer(m, i + 1, 1).astype(f32)
                    part = y[g * wide:(g + 1) * wide, p * LANES:(p + 1) * LANES]
                    h1[m, pl.ds(PAD + i * wide, wide), :] = part + own + bias0
            return 0
        lax.fori_loop(0, pairs0 // step0, first, 0)

    def clear_edges(ref, count, width, edge, off, side):
        z = jnp.zeros((edge * width, LANES), f32)
        zc = jnp.zeros((side, LANES), f32)

        @pl.when(i0 == 0)
        def _():
            ref[pl.ds(off, edge * width), :] = z

        @pl.when(i0 + tr == bins)
        def _():
            ref[pl.ds(off + (count - edge) * width, edge * width), :] = z

        @pl.when(j0 == 0)
        def _():
            for i in range(count):
                ref[pl.ds(off + i * width, side), :] = zc

        @pl.when(j0 + tc == bins)
        def _():
            for i in range(count):
                ref[pl.ds(off + (i + 1) * width - side, side), :] = zc

    for m in range(2):
        clear_edges(h1.at[m], tr + 12, wide, 6, PAD, 8)

    groups1 = (tr + 8) // 4
    step1 = pick(groups1, 3)

    def second(c, _):
        base = c * step1
        rows = [4 * (base + g) + e for g in range(step1) for e in range(2)]
        lhs = []
        for m in range(2):
            for q in range(4):
                for b in range(3):
                    cut = jnp.concatenate([
                        h1[m, pl.ds(PAD + (r + 2 * q) * wide + 4 + 2 * (b - 1), span), :]
                        for r in rows], axis=0)
                    lhs.append(jnp.maximum(cut, 0.0).astype(bf16))
        y = lax.dot_general(jnp.concatenate(lhs, axis=1), w1[...], NT,
                            preferred_element_type=f32)
        for k, r in enumerate(rows):
            for p in range(2):
                at = PAD + (r + 2 + 2 * p) * wide + 4
                both = h1[0, pl.ds(at, span), :] + h1[1, pl.ds(at, span), :]
                part = y[k * span:(k + 1) * span, p * LANES:(p + 1) * LANES]
                sym[pl.ds((r + 2 * p) * span, span), :] = (part + both) * 0.5 + bias1
        return 0

    lax.fori_loop(0, groups1 // step1, second, 0)
    clear_edges(sym, tr + 8, span, 4, 0, 4)

    groups2 = tr // 8
    for_rows = 2 if groups2 % 2 == 0 else 1

    def third(c, _):
        rows = [8 * (c * for_rows + g) + e for g in range(for_rows) for e in range(4)]
        cells = []
        for r in rows:
            line = []
            for q in range(4):
                for b in range(3):
                    cut = sym[pl.ds((r + 4 * q) * span + 4 * b, tc), :]
                    line.append(jnp.maximum(cut, 0.0).astype(bf16))
            for p in range(2):
                line.append(sym[pl.ds((r + 4 + 4 * p) * span + 4, tc), :].astype(bf16))
            cells.append(jnp.concatenate(line, axis=1))
        y = lax.dot_general(w2[...], jnp.concatenate(cells, axis=0), NT,
                            preferred_element_type=f32)
        for k, r in enumerate(rows):
            for p in range(2):
                part = y[p * ch:(p + 1) * ch, k * tc:(k + 1) * tc]
                acc[pl.ds(r + 4 * p, ch, stride=tr), :] = part + bias2
        return 0

    lax.fori_loop(0, groups2 // for_rows, third, 0)
    out_ref[...] = acc[...].reshape(ch, tr, tc).astype(out_ref.dtype)


def decode(terms, w, bias, tr, tc):
    bins = terms.shape[0]
    ch = w.shape[2]
    f32, bf16 = jnp.float32, jnp.bfloat16
    vm = pl.BlockSpec(memory_space=pltpu.VMEM)
    return pl.pallas_call(
        functools.partial(decoder_kernel, tr, tc),
        out_shape=jax.ShapeDtypeStruct((ch, tr, tc), bf16),
        in_specs=[vm, vm, vm],
        out_specs=vm,
        scratch_shapes=[
            pltpu.VMEM((bins + 2 * PAD, LANES), f32),
            pltpu.VMEM((bins + 2 * PAD, LANES), f32),
            pltpu.VMEM((2, 3, tc + 16, LANES), bf16),
            pltpu.VMEM((2, tr + 14, 16, LANES), bf16),
            pltpu.VMEM((2, 2 * LANES, 12 * LANES), bf16),
            pltpu.VMEM((2 * LANES, 24 * LANES), bf16),
            pltpu.VMEM((2 * ch, 14 * LANES), bf16),
            pltpu.VMEM((2, (tr + 12) * (tc + 16) + 2 * PAD, LANES), f32),
            pltpu.VMEM(((tr + 8) * (tc + 8), LANES), f32),
            pltpu.VMEM((ch * tr, LANES), f32),
        ],
    )(terms, w, bias)


def project_kernel(bins_ref, row_ref, col_ref, send_ref):
    ch = row_ref.shape[0]
    halves = []
    for w_ref in (row_ref, col_ref):
        part = lax.dot_general(bins_ref[...], w_ref[...], NT,
                               preferred_element_type=jnp.float32)
        blank = jnp.zeros((part.shape[0], LANES - ch), jnp.float32)
        halves.append(jnp.concatenate([part, blank], axis=1))
    both = jnp.concatenate(halves, axis=1).astype(send_ref.dtype)
    for k in range(send_ref.shape[0]):
        send_ref[k] = both


def project(bins, row_proj, col_proj, peers):
    vm = pl.BlockSpec(memory_space=pltpu.VMEM)
    return pl.pallas_call(
        project_kernel,
        out_shape=jax.ShapeDtypeStruct((peers, bins.shape[0], 2 * LANES), jnp.bfloat16),
        in_specs=[vm, vm, vm],
        out_specs=vm,
    )(bins, row_proj, col_proj)


def shards(bins, row_proj, col_proj, conv_weight, conv_bias):
    rows = lax.axis_size("row")
    cols = lax.axis_size("col")
    reps = lax.axis_size("rep")
    part = conv_bias.shape[1]
    if reps > 1:
        row_proj = lax.all_gather(row_proj, "rep", axis=0, tiled=True)
        col_proj = lax.all_gather(col_proj, "rep", axis=0, tiled=True)
        conv_weight = lax.all_gather(conv_weight, "rep", axis=2, tiled=True)
        conv_bias = lax.all_gather(conv_bias, "rep", axis=1, tiled=True)
    peers = rows * cols
    total = bins.shape[0] * peers
    send = project(bins, row_proj, col_proj, peers)
    terms = lax.all_to_all(send, ("row", "col"), 0, 0, tiled=True)
    terms = terms.reshape(total, 2 * LANES)
    bias = jnp.pad(conv_bias, ((0, 0), (0, LANES - conv_bias.shape[1])))
    out = decode(terms, conv_weight, bias, total // rows, total // cols)
    if reps > 1:
        out = lax.dynamic_slice_in_dim(out, lax.axis_index("rep") * part, part, 0)
    return out


def solution(mesh):
    placed = (
        P(("groups", "row", "col"), None),
        P("rep", None),
        P("rep", None),
        P(None, None, "rep", None),
        P(None, "rep"),
    )
    return jax.shard_map(
        shards,
        mesh=mesh,
        in_specs=placed,
        out_specs=P("rep", ("groups", "row"), "col"),
        check_vma=False,
    )
```

time: 195 us -> 30 us (0.15)
  blocking collectives: 134 us -> 0 us
  matrix products: 17.8 us -> 0 us
  starting transfers between devices: 21.7 us -> 7.33 us
  Pallas kernels: 0 us -> 13.2 us
  waiting for transfers between devices: 15.5 us -> 8.01 us
    all_gather x2 -> x0, blocking collectives: 134 us -> none  [the longest x1 70.1 us: shards(): lax.all_gather(col_local, ('row', 'col'), axis=0, tiled=True)]
    ppermute x12 -> x0, starting transfers between devices: 21.7 us -> none  [the longest x6 13.7 us: with_halo(): before = lax.ppermute(last, axis, up)]
    dot_general x47 -> x0, matrix products: 17.8 us -> none  [the longest x45 15.7 us: conv_valid(): jnp.einsum('oi,ipq->opq', filters[tap], window, preferred_element_type=jn...]
    ppermute x12 -> x0, waiting for transfers between devices: 15.5 us -> none  [the longest x6 15.5 us: with_halo(): after = lax.ppermute(leading, axis, down)]
    pallas_call x0 -> x2, Pallas kernels: none -> 13.2 us  [the longest x1 11.2 us: decode(): pl.pallas_call(functools.partial(decoder_kernel, tr, tc), out_shape=jax.S...]
    all_to_all x0 -> x1, waiting for transfers between devices: none -> 8.01 us  [shards(): terms = lax.all_to_all(send, ('row', 'col'), 0, 0, tiled=True)]
    all_to_all x0 -> x1, starting transfers between devices: none -> 7.33 us  [shards(): terms = lax.all_to_all(send, ('row', 'col'), 0, 0, tiled=True)]
  transfers between devices with their start and end apart: 12 -> 1, of which waited for: 5 -> 1; matrix products, arithmetic and copies ran while one was open for 5% -> 2% of each run, Pallas kernels for 0% -> 0%
where the time goes in v1:
time: 30 us; the launch traced here: 29.8 us
  Pallas kernels  13.2 us (44%)
  waiting for transfers between devices  8.01 us (27%)
  starting transfers between devices  7.33 us (24%)
  local copies, waits for them, and re-layouts  1.23 us (4%)
    pallas_call x1, Pallas kernels, decode(): pl.pallas_call(functools.partial(decoder_kernel, tr, tc), out_shape=jax.S...  11.2 us
    all_to_all x1, waiting for transfers between devices, shards(): terms = lax.all_to_all(send, ('row', 'col'), 0, 0, tiled=True)  8.01 us
    all_to_all x1, starting transfers between devices, shards(): terms = lax.all_to_all(send, ('row', 'col'), 0, 0, tiled=True)  7.33 us
    pallas_call x1, Pallas kernels, project(): pl.pallas_call(project_kernel, out_shape=jax.ShapeDtypeStruct((peers, bin...  2 us
    unnamed x4, local copies, waits for them, and re-layouts  0.65 us
  transfers between devices with their start and end apart: 1, of which 1 were waited for; matrix products, arithmetic and copies ran while one was open for 2% of the time, Pallas kernels for 0%

profile of v1, /device:TPU:0, one launch (start us, length us, event | category | flops | bytes accessed | tf_op | source)
XLA Modules:
  0.0 29.8 jit_solution(6010097286240076503)
XLA Ops:
  0.0 2.0 %shard_map.55 = bf16[32,8,256]{2,1,0:T(8,128)(2,1)} custom-call(bf16[8,1536]{1,0:T(8,128)(2,1)} %bins_ref.1, bf16[96,1536]{1,0:T(8,128)(2,1)} %row_ref.1, bf16[96,1536]{1,0:T(8,128)(2,1)} %col_ref.1), custom_call_target="tpu_custom_call" | custom-call | tf_op jit(solution)/shard_map/pallas_call | solution.py:209
  2.0 0.0 copy-start.1
  2.0 7.3 %all-to-all-start = ((bf16[32,8,256]{2,1,0:T(8,128)(2,1)}), bf16[32,8,256]{2,1,0:T(8,128)(2,1)S(1)}, u32[]{:S(2)}, u32[]{:S(2)}) async-start(bf16[32,8,256]{2,1,0:T(8,128)(2,1)} %shard_map.55), calls=%async_computation | async-start | bytes 262144 | tf_op jit(solution)/shard_map/all_to_all | solution.py:230
  9.3 0.0 copy-done.1
  9.3 0.6 %pad.4.bias_ref = f32[3,128]{1,0:T(4,128)} pad(f32[3,96]{1,0:T(4,128)S(1)} %copy-done.1, f32[]{:T(128)} %constant.2.clone.1), padding=0_0x0_32 | pad | bytes 2692 | tf_op jit(solution)/shard_map/jit(_pad)/pad | solution.py:232
  9.9 8.0 %all-to-all-done = bf16[32,8,256]{2,1,0:T(8,128)(2,1)S(1)} async-done(((bf16[32,8,256]{2,1,0:T(8,128)(2,1)}), bf16[32,8,256]{2,1,0:T(8,128)(2,1)S(1)}, u32[]{:S(2)}, u32[]{:S(2)}) %all-to-all-start) | async-done | bytes 131104 | tf_op jit(solution)/shard_map/all_to_all | solution.py:230
  17.9 0.0 copy-start
  17.9 0.6 %copy-done = bf16[32,8,256]{2,1,0:T(8,128)(2,1)} copy-done((bf16[32,8,256]{2,1,0:T(8,128)(2,1)}, bf16[32,8,256]{2,1,0:T(8,128)(2,1)S(1)}, u32[]{:S(2)}) %copy-start) | copy-done | bytes 131096
  18.6 11.2 %shard_map.56 = bf16[96,16,128]{2,1,0:T(8,128)(2,1)} custom-call(bf16[256,256]{1,0:T(8,128)(2,1)} %bitcast.1, bf16[3,9,96,96]{3,2,1,0:T(8,128)(2,1)} %w_ref.1, f32[3,128]{1,0:T(4,128)} %pad.4.bias_ref), custom_call_target="tpu_custom_call" | custom-call | tf_op jit(solution)/shard_map/pallas_call | solution.py:174
Async XLA Ops:
  2.0 7.3 %copy-start.1 = (f32[3,96]{1,0:T(4,128)S(1)}, f32[3,96]{1,0:T(4,128)}, u32[]{:S(2)}) copy-start(f32[3,96]{1,0:T(4,128)} %param.9) | copy-start | bytes 3460
  2.0 15.9 %all-to-all-start = ((bf16[32,8,256]{2,1,0:T(8,128)(2,1)}), bf16[32,8,256]{2,1,0:T(8,128)(2,1)S(1)}, u32[]{:S(2)}, u32[]{:S(2)}) async-start(bf16[32,8,256]{2,1,0:T(8,128)(2,1)} %shard_map.55), calls=%async_computation | async-start | bytes 262144 | tf_op jit(solution)/shard_map/all_to_all | solution.py:230
  17.9 0.6 %copy-start = (bf16[32,8,256]{2,1,0:T(8,128)(2,1)}, bf16[32,8,256]{2,1,0:T(8,128)(2,1)S(1)}, u32[]{:S(2)}) copy-start(bf16[32,8,256]{2,1,0:T(8,128)(2,1)S(1)} %all-to-all-done) | copy-start | bytes 393220

commit v2 on v1

--- a/solution.py
+++ b/solution.py
@@ -7,7 +7,15 @@
 from jax.sharding import PartitionSpec as P
 
 LANES = 128
+FRONT_BYTES = 48 << 20
+DECODE_BYTES = 40 << 20
 PAD = 16
+WIDTH = 12 * LANES
+DIRECT0 = 0
+MIRROR0 = WIDTH
+BOTH1 = 2 * WIDTH
+PACKED = 4 * WIDTH
+LAST = WIDTH + 2 * LANES
 NT = (((1,), (1,)), ((), ()))
 
 
@@ -15,24 +23,10 @@
     return max(k for k in range(1, min(count, most) + 1) if count % k == 0)
 
 
-def decoder_kernel(tr, tc, terms_ref, w_ref, bias_ref, out_ref,
-                   rows_f, cols_f, vtab, utab, w0, w1, w2, h1, sym, acc):
-    bins = terms_ref.shape[0]
+def filters_kernel(w_ref, b_ref, packed, taps_ref, bias_ref, column_ref):
     ch = w_ref.shape[2]
-    wide = tc + 16
-    span = tc + 8
-    i0 = lax.axis_index("row") * tr
-    j0 = lax.axis_index("col") * tc
     f32, bf16 = jnp.float32, jnp.bfloat16
-
-    for tab, lo in ((rows_f, 0), (cols_f, LANES)):
-        tab[0:PAD] = jnp.zeros((PAD, LANES), f32)
-        tab[PAD + bins:] = jnp.zeros((PAD, LANES), f32)
-        tab[PAD:PAD + bins] = terms_ref[:, lo:lo + LANES].astype(f32)
-
-    w0[...] = jnp.zeros(w0.shape, bf16)
-    w1[...] = jnp.zeros(w1.shape, bf16)
-    w2[...] = jnp.zeros(w2.shape, bf16)
+    packed[...] = jnp.zeros(packed.shape, bf16)
     for q in range(4):
         for b in range(3):
             at = (q * 3 + b) * LANES
@@ -40,21 +34,44 @@
                 a = q - p
                 if 0 <= a < 3:
                     rows = slice(p * LANES, p * LANES + ch)
-                    w0[0, rows, at:at + ch] = w_ref[0, 3 * a + b]
-                    w0[1, rows, at:at + ch] = w_ref[0, 3 * b + a]
-                    w1[rows, at:at + ch] = w_ref[1, 3 * a + b]
-                    w1[rows, 12 * LANES + at:12 * LANES + at + ch] = w_ref[1, 3 * b + a]
-                    w2[p * ch:(p + 1) * ch, at:at + ch] = w_ref[2, 3 * a + b]
+                    for first, layer, tap in (
+                        (DIRECT0, 0, 3 * a + b),
+                        (MIRROR0, 0, 3 * b + a),
+                        (BOTH1, 1, 3 * a + b),
+                        (BOTH1 + WIDTH, 1, 3 * b + a),
+                    ):
+                        packed[rows, first + at:first + at + ch] = w_ref[layer, tap]
+    taps_ref[...] = jnp.zeros(taps_ref.shape, bf16)
+    for tap in range(9):
+        taps_ref[:, tap * LANES:tap * LANES + ch] = w_ref[2, tap]
     eye = (lax.broadcasted_iota(jnp.int32, (ch, LANES), 0)
            == lax.broadcasted_iota(jnp.int32, (ch, LANES), 1))
     unit = jnp.where(eye, 1.0, 0.0)
-    for p in range(2):
-        at = (12 + p) * LANES
-        w2[p * ch:(p + 1) * ch, at:at + LANES] = unit.astype(bf16)
+    blank = jnp.zeros((b_ref.shape[0], LANES - ch), f32)
+    bias = jnp.concatenate([b_ref[...], blank], axis=1)
+    bias_ref[...] = bias
+    column_ref[...] = jnp.broadcast_to(
+        jnp.sum(unit * bias[2:3, :], axis=1, keepdims=True), (ch, LANES))
+
+
+def decoder_kernel(tr, tc, terms_ref, packed, taps_ref, bias_ref, column_ref, out_ref,
+                   rows_f, cols_f, vtab, utab, h1, sym, acc, last):
+    bins = terms_ref.shape[0]
+    wide = tc + 16
+    span = tc + 8
+    i0 = lax.axis_index("row") * tr
+    j0 = lax.axis_index("col") * tc
+    f32, bf16 = jnp.float32, jnp.bfloat16
+
+    for tab, lo in ((rows_f, 0), (cols_f, LANES)):
+        tab[0:PAD] = jnp.zeros((PAD, LANES), f32)
+        tab[PAD + bins:] = jnp.zeros((PAD, LANES), f32)
+        tab[PAD:PAD + bins] = terms_ref[:, lo:lo + LANES].astype(f32)
+
     bias0 = bias_ref[0:1, :]
     bias1 = bias_ref[1:2, :]
-    bias2 = jnp.broadcast_to(
-        jnp.sum(unit * bias_ref[2:3, :], axis=1, keepdims=True), (ch, LANES))
+    ch = out_ref.shape[0]
+    bias2 = column_ref[...]
 
     for m, (utab_f, vtab_f) in enumerate(((rows_f, cols_f), (cols_f, rows_f))):
         for b in range(3):
@@ -77,7 +94,7 @@
                     jnp.maximum(outer(m, 2 * (base + g) + q, b), 0)
                     for q in range(4) for b in range(3)], axis=1)
                 for g in range(step0)], axis=0)
-            y = lax.dot_general(lhs, w0[m], NT, preferred_element_type=f32)
+            y = lax.dot_general(lhs, packed[:, m * WIDTH:(m + 1) * WIDTH], NT, preferred_element_type=f32)
             for g in range(step0):
                 for p in range(2):
                     i = 2 * (base + g) + p
@@ -126,7 +143,7 @@
                         h1[m, pl.ds(PAD + (r + 2 * q) * wide + 4 + 2 * (b - 1), span), :]
                         for r in rows], axis=0)
                     lhs.append(jnp.maximum(cut, 0.0).astype(bf16))
-        y = lax.dot_general(jnp.concatenate(lhs, axis=1), w1[...], NT,
+        y = lax.dot_general(jnp.concatenate(lhs, axis=1), packed[:, BOTH1:PACKED], NT,
                             preferred_element_type=f32)
         for k, r in enumerate(rows):
             for p in range(2):
@@ -139,6 +156,15 @@
     lax.fori_loop(0, groups1 // step1, second, 0)
     clear_edges(sym, tr + 8, span, 4, 0, 4)
 
+    last[...] = jnp.zeros(last.shape, bf16)
+    eye = (lax.broadcasted_iota(jnp.int32, (ch, LANES), 0)
+           == lax.broadcasted_iota(jnp.int32, (ch, LANES), 1))
+    for p in range(2):
+        rows = slice(p * ch, (p + 1) * ch)
+        at = 3 * p * LANES
+        last[rows, at:at + 9 * LANES] = taps_ref[...]
+        at = WIDTH + p * LANES
+        last[rows, at:at + LANES] = jnp.where(eye, 1.0, 0.0).astype(bf16)
     groups2 = tr // 8
     for_rows = 2 if groups2 % 2 == 0 else 1
 
@@ -154,7 +180,7 @@
             for p in range(2):
                 line.append(sym[pl.ds((r + 4 + 4 * p) * span + 4, tc), :].astype(bf16))
             cells.append(jnp.concatenate(line, axis=1))
-        y = lax.dot_general(w2[...], jnp.concatenate(cells, axis=0), NT,
+        y = lax.dot_general(last[...], jnp.concatenate(cells, axis=0), NT,
                             preferred_element_type=f32)
         for k, r in enumerate(rows):
             for p in range(2):
@@ -166,51 +192,81 @@
     out_ref[...] = acc[...].reshape(ch, tr, tc).astype(out_ref.dtype)
 
 
-def decode(terms, w, bias, tr, tc):
-    bins = terms.shape[0]
+def filters(w, bias):
     ch = w.shape[2]
     f32, bf16 = jnp.float32, jnp.bfloat16
     vm = pl.BlockSpec(memory_space=pltpu.VMEM)
+    shapes = (
+        ((2 * LANES, PACKED), bf16),
+        ((ch, 9 * LANES), bf16),
+        ((bias.shape[0], LANES), f32),
+        ((ch, LANES), f32),
+    )
+    return pl.pallas_call(
+        filters_kernel,
+        out_shape=[jax.ShapeDtypeStruct(*s) for s in shapes],
+        in_specs=[vm, vm],
+        out_specs=[vm] * len(shapes),
+        compiler_params=pltpu.CompilerParams(vmem_limit_bytes=FRONT_BYTES),
+        cost_estimate=pl.CostEstimate(flops=0, bytes_accessed=8 << 20, transcendentals=0),
+    )(w, bias)
+
+
+def decode(terms, packed, tr, tc):
+    bins = terms.shape[0]
+    ch = packed[1].shape[0]
+    f32, bf16 = jnp.float32, jnp.bfloat16
+    vm = pl.BlockSpec(memory_space=pltpu.VMEM)
+    scratch = (
+        ((bins + 2 * PAD, LANES), f32),
+        ((bins + 2 * PAD, LANES), f32),
+        ((2, 3, tc + 16, LANES), bf16),
+        ((2, tr + 14, 16, LANES), bf16),
+        ((2, (tr + 12) * (tc + 16) + 2 * PAD, LANES), f32),
+        (((tr + 8) * (tc + 8), LANES), f32),
+        ((ch * tr, LANES), f32),
+        ((2 * ch, LAST), bf16),
+    )
     return pl.pallas_call(
         functools.partial(decoder_kernel, tr, tc),
         out_shape=jax.ShapeDtypeStruct((ch, tr, tc), bf16),
-        in_specs=[vm, vm, vm],
+        in_specs=[vm] * 5,
         out_specs=vm,
-        scratch_shapes=[
-            pltpu.VMEM((bins + 2 * PAD, LANES), f32),
-            pltpu.VMEM((bins + 2 * PAD, LANES), f32),
-            pltpu.VMEM((2, 3, tc + 16, LANES), bf16),
-            pltpu.VMEM((2, tr + 14, 16, LANES), bf16),
-            pltpu.VMEM((2, 2 * LANES, 12 * LANES), bf16),
-            pltpu.VMEM((2 * LANES, 24 * LANES), bf16),
-            pltpu.VMEM((2 * ch, 14 * LANES), bf16),
-            pltpu.VMEM((2, (tr + 12) * (tc + 16) + 2 * PAD, LANES), f32),
-            pltpu.VMEM(((tr + 8) * (tc + 8), LANES), f32),
-            pltpu.VMEM((ch * tr, LANES), f32),
-        ],
-    )(terms, w, bias)
-
-
-def project_kernel(bins_ref, row_ref, col_ref, send_ref):
-    ch = row_ref.shape[0]
-    halves = []
-    for w_ref in (row_ref, col_ref):
-        part = lax.dot_general(bins_ref[...], w_ref[...], NT,
-                               preferred_element_type=jnp.float32)
-        blank = jnp.zeros((part.shape[0], LANES - ch), jnp.float32)
-        halves.append(jnp.concatenate([part, blank], axis=1))
-    both = jnp.concatenate(halves, axis=1).astype(send_ref.dtype)
+        scratch_shapes=[pltpu.VMEM(*s) for s in scratch],
+        compiler_params=pltpu.CompilerParams(vmem_limit_bytes=DECODE_BYTES),
+    )(terms, *packed)
+
+
+def project_kernel(bins_hbm, row_hbm, col_hbm, send_ref, bins, w, sems):
+    ch = row_hbm.shape[0]
+    copies = [
+        pltpu.make_async_copy(row_hbm, w.at[0:ch], sems.at[0]),
+        pltpu.make_async_copy(col_hbm, w.at[LANES:LANES + ch], sems.at[1]),
+        pltpu.make_async_copy(bins_hbm, bins, sems.at[2]),
+    ]
+    for copy in copies:
+        copy.start()
+    for p in range(2):
+        w[p * LANES + ch:(p + 1) * LANES] = jnp.zeros((LANES - ch, w.shape[1]), w.dtype)
+    for copy in copies:
+        copy.wait()
+    both = lax.dot_general(bins[...], w[...], NT, preferred_element_type=jnp.float32)
+    both = both.astype(send_ref.dtype)
     for k in range(send_ref.shape[0]):
         send_ref[k] = both
 
 
 def project(bins, row_proj, col_proj, peers):
-    vm = pl.BlockSpec(memory_space=pltpu.VMEM)
     return pl.pallas_call(
         project_kernel,
         out_shape=jax.ShapeDtypeStruct((peers, bins.shape[0], 2 * LANES), jnp.bfloat16),
-        in_specs=[vm, vm, vm],
-        out_specs=vm,
+        in_specs=[pl.BlockSpec(memory_space=pltpu.HBM)] * 3,
+        out_specs=pl.BlockSpec(memory_space=pltpu.VMEM),
+        scratch_shapes=[
+            pltpu.VMEM(bins.shape, bins.dtype),
+            pltpu.VMEM((2 * LANES, bins.shape[1]), bins.dtype),
+            pltpu.SemaphoreType.DMA((3,)),
+        ],
     )(bins, row_proj, col_proj)
 
 
@@ -229,8 +285,8 @@
     send = project(bins, row_proj, col_proj, peers)
     terms = lax.all_to_all(send, ("row", "col"), 0, 0, tiled=True)
     terms = terms.reshape(total, 2 * LANES)
-    bias = jnp.pad(conv_bias, ((0, 0), (0, LANES - conv_bias.shape[1])))
-    out = decode(terms, conv_weight, bias, total // rows, total // cols)
+    packed = filters(conv_weight, conv_bias)
+    out = decode(terms, packed, total // rows, total // cols)
     if reps > 1:
         out = lax.dynamic_slice_in_dim(out, lax.axis_index("rep") * part, part, 0)
     return out

time: 30 us -> 27.8 us (0.927)
  waiting for transfers between devices: 8.01 us -> 6.29 us
  Pallas kernels: 13.2 us -> 12.2 us
  local copies, waits for them, and re-layouts: 1.23 us -> 1.77 us
    all_to_all x1, waiting for transfers between devices: 8.01 us -> 6.29 us  [shards(): terms = lax.all_to_all(send, ('row', 'col'), 0, 0, tiled=True)]
    pallas_call x1, Pallas kernels: 11.2 us -> 9.58 us  [decode(): pl.pallas_call(functools.partial(decoder_kernel, tr, tc), out_shape=jax.S...]
    unnamed x4, local copies, waits for them, and re-layouts: 0.65 us -> 1.77 us
    pad x1 -> x0, local copies, waits for them, and re-layouts: 0.58 us -> none  [shards(): bias = jnp.pad(conv_bias, ((0, 0), (0, LANES - conv_bias.shape[1])))]
    pallas_call x0 -> x1, Pallas kernels: none -> 0.52 us  [filters(): pl.pallas_call(filters_kernel, out_shape=[jax.ShapeDtypeStruct(*s) for s...]
  transfers between devices with their start and end apart: 1 -> 1, of which waited for: 1 -> 1; matrix products, arithmetic and copies ran while one was open for 2% -> 0% of each run, Pallas kernels for 0% -> 2%
where the time goes in v2:
time: 27.8 us; the launch traced here: 27.6 us
  Pallas kernels  12.2 us (44%)
  starting transfers between devices  7.33 us (26%)
  waiting for transfers between devices  6.29 us (23%)
  local copies, waits for them, and re-layouts  1.77 us (6%)
    pallas_call x1, Pallas kernels, decode(): pl.pallas_call(functools.partial(decoder_kernel, tr, tc), out_shape=jax.S...  9.58 us
    all_to_all x1, starting transfers between devices, shards(): terms = lax.all_to_all(send, ('row', 'col'), 0, 0, tiled=True)  7.33 us
    all_to_all x1, waiting for transfers between devices, shards(): terms = lax.all_to_all(send, ('row', 'col'), 0, 0, tiled=True)  6.29 us
    pallas_call x1, Pallas kernels, project(): pl.pallas_call(project_kernel, out_shape=jax.ShapeDtypeStruct((peers, bin...  2.06 us
    unnamed x4, local copies, waits for them, and re-layouts  1.77 us
  transfers between devices with their start and end apart: 1, of which 1 were waited for; matrix products, arithmetic and copies ran while one was open for 0% of the time, Pallas kernels for 2%

profile of v2, /device:TPU:0, one launch (start us, length us, event | category | flops | bytes accessed | tf_op | source)
XLA Modules:
  0.0 27.6 jit_solution(15008431213877168144)
XLA Ops:
  0.0 2.1 %shard_map.55 = bf16[32,8,256]{2,1,0:T(8,128)(2,1)} custom-call(bf16[8,1536]{1,0:T(8,128)(2,1)} %bins_hbm.1, bf16[96,1536]{1,0:T(8,128)(2,1)} %row_hbm.1, bf16[96,1536]{1,0:T(8,128)(2,1)} %col_hbm.1), custom_call_target="tpu_custom_call" | custom-call | tf_op jit(solution)/shard_map/pallas_call | solution.py:260
  2.1 7.3 %all-to-all-start = ((bf16[32,8,256]{2,1,0:T(8,128)(2,1)}), bf16[32,8,256]{2,1,0:T(8,128)(2,1)S(1)}, u32[]{:S(2)}, u32[]{:S(2)}) async-start(bf16[32,8,256]{2,1,0:T(8,128)(2,1)} %shard_map.55), calls=%async_computation | async-start | bytes 262144 | tf_op jit(solution)/shard_map/all_to_all | solution.py:286
  9.4 0.0 copy-start
  9.4 1.1 %copy-done = bf16[3,9,96,96]{3,2,1,0:T(8,128)(2,1)S(1)} copy-done((bf16[3,9,96,96]{3,2,1,0:T(8,128)(2,1)S(1)}, bf16[3,9,96,96]{3,2,1,0:T(8,128)(2,1)}, u32[]{:S(2)}) %copy-start) | copy-done | bytes 497688
  10.5 0.0 copy-start.1
  10.5 0.7 %copy-done.1 = f32[3,96]{1,0:T(4,128)S(1)} copy-done((f32[3,96]{1,0:T(4,128)S(1)}, f32[3,96]{1,0:T(4,128)}, u32[]{:S(2)}) %copy-start.1) | copy-done | bytes 1176
  11.2 0.5 %shard_map.56 = (bf16[256,6144]{1,0:T(8,128)(2,1)S(1)}, bf16[96,1152]{1,0:T(8,128)(2,1)S(1)}, f32[3,128]{1,0:T(4,128)S(1)}, f32[96,128]{1,0:T(8,128)S(1)}) custom-call(bf16[3,9,96,96]{3,2,1,0:T(8,128)(2,1)S(1)} %copy-done, f32[3,96]{1,0:T(4,128)S(1)} %copy-done.1), custom_call_target="tpu_custom_call" | custom-call | bytes 8388608 | tf_op jit(solution)/shard_map/pallas_call | solution.py:205
  11.7 6.3 %all-to-all-done = bf16[32,8,256]{2,1,0:T(8,128)(2,1)S(1)} async-done(((bf16[32,8,256]{2,1,0:T(8,128)(2,1)}), bf16[32,8,256]{2,1,0:T(8,128)(2,1)S(1)}, u32[]{:S(2)}, u32[]{:S(2)}) %all-to-all-start) | async-done | bytes 131104 | tf_op jit(solution)/shard_map/all_to_all | solution.py:286
  18.0 9.6 %shard_map.57 = bf16[96,16,128]{2,1,0:T(8,128)(2,1)} custom-call(bf16[256,256]{1,0:T(8,128)(2,1)S(1)} %bitcast.1, bf16[256,6144]{1,0:T(8,128)(2,1)S(1)} %get-tuple-element.9.packed, bf16[96,1152]{1,0:T(8,128)(2,1)S(1)} %get-tuple-element.10.taps_ref, f32[3,128]{1,0:T(4,128)S(1)} %get-tuple-element.11.bias_ref, f32[96,128]{1,0:T(8,128)S(1)} %get-tuple-element.12.column_ref), custom_call_target="tpu_custom_call" | custom-call | tf_op jit(solution)/shard_map/pallas_call | solution.py:230
Async XLA Ops:
  2.1 15.9 %all-to-all-start = ((bf16[32,8,256]{2,1,0:T(8,128)(2,1)}), bf16[32,8,256]{2,1,0:T(8,128)(2,1)S(1)}, u32[]{:S(2)}, u32[]{:S(2)}) async-start(bf16[32,8,256]{2,1,0:T(8,128)(2,1)} %shard_map.55), calls=%async_computation | async-start | bytes 262144 | tf_op jit(solution)/shard_map/all_to_all | solution.py:286
  9.4 1.1 %copy-start = (bf16[3,9,96,96]{3,2,1,0:T(8,128)(2,1)S(1)}, bf16[3,9,96,96]{3,2,1,0:T(8,128)(2,1)}, u32[]{:S(2)}) copy-start(bf16[3,9,96,96]{3,2,1,0:T(8,128)(2,1)} %w_ref.1) | copy-start | bytes 1492996
  10.5 0.7 %copy-start.1 = (f32[3,96]{1,0:T(4,128)S(1)}, f32[3,96]{1,0:T(4,128)}, u32[]{:S(2)}) copy-start(f32[3,96]{1,0:T(4,128)} %b_ref.1) | copy-start | bytes 3460

commit v3 on v2

v3 whole, which is shorter than its diff:
```python
import functools
import jax
import jax.numpy as jnp
from jax import lax
from jax.experimental import pallas as pl
from jax.experimental.pallas import tpu as pltpu
from jax.sharding import PartitionSpec as P

LANES = 128
PAD = 16
BLOCKS = 9
STEP0 = 4
STEP1 = 1
STEP2 = 1
APART = True
WIDTH = BLOCKS * LANES
FRONT_BYTES = 48 << 20
DECODE_BYTES = 40 << 20
NT = (((1,), (1,)), ((), ()))


def cuts(count, most):
    parts = -(-count // most)
    edges = [count * k // parts for k in range(parts + 1)]
    return list(zip(edges[:-1], edges[1:]))


def lane_ids(shape):
    return lax.broadcasted_iota(jnp.int32, shape, len(shape) - 1)


def third_of(value, ch, t):
    spare = LANES - ch
    return pltpu.roll(value, (ch - t * spare) % LANES, value.ndim - 1)


def filters_kernel(w_ref, b_ref, packed0, packed1, last, bias_ref, column_ref, wide):
    ch = w_ref.shape[2]
    spare = LANES - ch
    f32, bf16 = jnp.float32, jnp.bfloat16
    wide[...] = jnp.zeros(wide.shape, f32)

    def fill(ref, rows0, rows1, first, layer, swap):
        for b in range(3):
            taps = []
            for a in range(3):
                wide[:, 0:ch] = w_ref[layer, 3 * b + a if swap else 3 * a + b].astype(f32)
                taps.append(wide[...])
            for t in range(3):
                cols = slice(first + (3 * t + b) * LANES, first + (3 * t + b + 1) * LANES)
                ref[rows0, cols] = taps[t].astype(bf16)
                main = taps[t - 1] if t else jnp.zeros((ch, LANES), f32)
                moved = third_of(taps[2], ch, t)
                ref[rows1, cols] = jnp.where(lane_ids((ch, LANES)) < ch, main, moved).astype(bf16)

    low, high = slice(0, ch), slice(LANES, LANES + ch)
    for ref in (packed0, packed1):
        for p in range(2):
            ref[p * LANES + ch:(p + 1) * LANES] = jnp.zeros((spare, ref.shape[1]), bf16)
    fill(packed0, low, high, 0, 0, False)
    fill(packed0, low, high, WIDTH, 0, True)
    fill(packed1, low, high, 0, 1, False)
    fill(packed1, low, high, WIDTH, 1, True)
    fill(last, slice(0, ch), slice(ch, 2 * ch), 0, 2, False)
    eye = lax.broadcasted_iota(jnp.int32, (ch, LANES), 0) == lane_ids((ch, LANES))
    unit = jnp.where(eye, 1.0, 0.0)
    for p in range(2):
        for s in range(2):
            part = unit if p == s else jnp.zeros((ch, LANES), f32)
            last[p * ch:(p + 1) * ch, WIDTH + s * LANES:WIDTH + (s + 1) * LANES] = part.astype(bf16)
    blank = jnp.zeros((b_ref.shape[0], spare), f32)
    bias = jnp.concatenate([b_ref[...], blank], axis=1)
    bias_ref[...] = bias
    column_ref[...] = jnp.broadcast_to(
        jnp.sum(unit * bias[2:3, :], axis=1, keepdims=True), (ch, LANES))


def decoder_kernel(tr, tc, terms_ref, packed0, packed1, last, bias_ref, column_ref, out_ref,
                   rows_f, cols_f, mixed_v, mixed_u, plain_v, plain_u, h1, sym, acc):
    bins = terms_ref.shape[0]
    ch = out_ref.shape[0]
    wide = tc + 16
    span = tc + 8
    f32, bf16 = jnp.float32, jnp.bfloat16
    i0 = lax.axis_index("row") * tr
    j0 = lax.axis_index("col") * tc
    top, bottom = i0 == 0, i0 + tr == bins
    left, right = j0 == 0, j0 + tc == bins
    bias0 = bias_ref[0:1, :]
    bias1 = bias_ref[1:2, :]

    def stage(body):
        if APART:
            pl.when(i0 >= 0)(body)
        else:
            body()

    for tab, lo in ((rows_f, 0), (cols_f, LANES)):
        tab[0:PAD] = jnp.zeros((PAD, LANES), f32)
        tab[PAD + bins:] = jnp.zeros((PAD, LANES), f32)
        tab[PAD:PAD + bins] = terms_ref[:, lo:lo + LANES].astype(f32)

    pairs0 = (tr + 12) // 2
    tall = mixed_u.shape[2]
    body_v = lane_ids((wide + 8, LANES)) < ch
    body_u = lane_ids((tall, LANES)) < ch
    for m, (u_src, v_src) in enumerate(((rows_f, cols_f), (cols_f, rows_f))):
        line = v_src[pl.ds(j0 + PAD - 9, wide + 8), :]
        plain_v[m] = line
        for t in range(3):
            mixed_v[m, t] = jnp.where(body_v, line, third_of(line, ch, t))
        fourth = u_src[pl.ds(i0 + PAD - 7 + 3, tall), :]
        for t in range(3):
            row = u_src[pl.ds(i0 + PAD - 7 + t, tall), :]
            mixed_u[m, t] = jnp.where(body_u, row, third_of(fourth, ch, t))
        plain_u[m] = u_src[pl.ds(i0 + PAD - 6, tall), :]

    def put(ref, where, k, value, width):
        at = k // 2 + 1
        cells = slice(0, width)
        if k % 2 == 0:
            ref[where + (at, 0, cells, slice(0, ch))] = value[:, 0:ch]
            ref[where + (at - 1, 2, cells, slice(0, ch))] = value[:, 0:ch]
        else:
            ref[where + (at, 1, cells, slice(0, ch))] = value[:, 0:ch]
            for t in range(3):
                ref[where + (at - 1, t, cells, slice(ch, LANES))] = third_of(value, ch, t)[:, ch:LANES]

    def clear(ref, heads, groups, width, side, deep):
        main, rest = slice(0, ch), slice(ch, LANES)
        body = jnp.zeros((width, ch), f32)
        tail = jnp.zeros((width, LANES - ch), f32)
        edge = jnp.zeros((side, LANES), f32)
        above = [(1, 0, main)] + ([(1, 1, main), (2, 0, main), (1, 2, main)] if deep == 3 else [])
        below = [(groups, t, rest) for t in range(3)]
        if deep == 3:
            below += [(groups, 1, main), (groups, 2, main)] + [(groups - 1, t, rest) for t in range(3)]
        for flag, places in ((top, above), (bottom, below)):
            @pl.when(flag)
            def _(places=places):
                for head in heads:
                    for at, t, lanes in places:
                        ref[head + (at, t, slice(0, width), lanes)] = body if lanes == main else tail
        for flag, start in ((left, 0), (right, width - side)):
            @pl.when(flag)
            def _(start=start):
                for head in heads:
                    for at in range(1, groups + 1):
                        for t in range(3):
                            ref[head + (at, t, slice(start, start + side), slice(0, LANES))] = edge

    def first(m, lo, hi):
        rows = []
        for n in range(lo, hi):
            line = []
            for t in range(3):
                u = jnp.broadcast_to(mixed_u[m, t, 2 * n:2 * n + 1, :], (wide, LANES)).astype(bf16)
                for b in range(3):
                    v = mixed_v[m, t, b:b + wide, :].astype(bf16)
                    line.append(jnp.maximum(v * u, 0))
            rows.append(jnp.concatenate(line, axis=1))
        y = lax.dot_general(jnp.concatenate(rows, axis=0), packed0[:, m * WIDTH:(m + 1) * WIDTH], NT,
                            preferred_element_type=f32)
        for k, n in enumerate(range(lo, hi)):
            for e in range(2):
                own = plain_v[m, 1:1 + wide, :] * plain_u[m, 2 * n + e:2 * n + e + 1, :]
                part = y[k * wide:(k + 1) * wide, e * LANES:(e + 1) * LANES]
                put(h1, (m, e), n, part + own + bias0, wide)

    for m in range(2):
        for lo, hi in cuts(pairs0, STEP0):
            stage(functools.partial(first, m, lo, hi))
    groups1 = (tr + 8) // 4
    clear(h1, [(m, e) for m in range(2) for e in range(2)], groups1, wide, 8, 3)

    def second(lo, hi):
        spots = [(k, e) for k in range(lo, hi) for e in range(2)]
        lhs = []
        for m in range(2):
            for t in range(3):
                for b in range(3):
                    cut = jnp.concatenate([
                        h1[m, e, k + 1, t, 2 + 2 * b:2 + 2 * b + span, :] for k, e in spots], axis=0)
                    lhs.append(jnp.maximum(cut.astype(bf16), 0))
        y = lax.dot_general(jnp.concatenate(lhs, axis=1), packed1[...], NT, preferred_element_type=f32)
        for s, (k, e) in enumerate(spots):
            for p in range(2):
                both = h1[0, e, k + 1, 1 + p, 4:4 + span, :] + h1[1, e, k + 1, 1 + p, 4:4 + span, :]
                part = y[s * span:(s + 1) * span, p * LANES:(p + 1) * LANES]
                put(sym, (e + 2 * p,), k, (part + both) * 0.5 + bias1, span)

    for lo, hi in cuts(groups1, STEP1):
        stage(functools.partial(second, lo, hi))
    groups2 = tr // 8
    clear(sym, [(e,) for e in range(4)], groups2, span, 4, 1)

    bias2 = column_ref[...]
    def third(lo, hi):
        spots = [(g, e) for g in range(lo, hi) for e in range(4)]
        cells = []
        for g, e in spots:
            line = []
            for t in range(3):
                for b in range(3):
                    line.append(jnp.maximum(sym[e, g + 1, t, 4 * b:4 * b + tc, :].astype(bf16), 0))
            for p in range(2):
                line.append(sym[e, g + 1, 1 + p, 4:4 + tc, :].astype(bf16))
            cells.append(jnp.concatenate(line, axis=1))
        y = lax.dot_general(last[...], jnp.concatenate(cells, axis=0), NT, preferred_element_type=f32)
        for s, (g, e) in enumerate(spots):
            for p in range(2):
                part = y[p * ch:(p + 1) * ch, s * tc:(s + 1) * tc]
                acc[pl.ds(8 * g + e + 4 * p, ch, stride=tr), :] = part + bias2

    for lo, hi in cuts(groups2, STEP2):
        stage(functools.partial(third, lo, hi))
    out_ref[...] = acc[...].reshape(ch, tr, tc).astype(out_ref.dtype)


def filters(w, bias):
    ch = w.shape[2]
    f32, bf16 = jnp.float32, jnp.bfloat16
    vm = pl.BlockSpec(memory_space=pltpu.VMEM)
    shapes = (
        ((2 * LANES, 2 * WIDTH), bf16),
        ((2 * LANES, 2 * WIDTH), bf16),
        ((2 * ch, WIDTH + 2 * LANES), bf16),
        ((bias.shape[0], LANES), f32),
        ((ch, LANES), f32),
    )
    return pl.pallas_call(
        filters_kernel,
        out_shape=[jax.ShapeDtypeStruct(*s) for s in shapes],
        in_specs=[vm, vm],
        out_specs=[vm] * len(shapes),
        scratch_shapes=[pltpu.VMEM((ch, LANES), f32)],
        compiler_params=pltpu.CompilerParams(vmem_limit_bytes=FRONT_BYTES),
        cost_estimate=pl.CostEstimate(flops=0, bytes_accessed=8 << 20, transcendentals=0),
    )(w, bias)


def decode(terms, packed, tr, tc):
    bins = terms.shape[0]
    ch = packed[4].shape[0]
    f32, bf16 = jnp.float32, jnp.bfloat16
    vm = pl.BlockSpec(memory_space=pltpu.VMEM)
    wide, span = tc + 16, tc + 8
    pairs0, groups1 = (tr + 12) // 2, (tr + 8) // 4
    tall = -(-(tr + 12) // 8) * 8
    scratch = (
        ((bins + 2 * PAD, LANES), f32),
        ((bins + 2 * PAD, LANES), f32),
        ((2, 3, wide + 8, LANES), f32),
        ((2, 3, tall, LANES), f32),
        ((2, wide + 8, LANES), f32),
        ((2, tall, LANES), f32),
        ((2, 2, pairs0 // 2 + 1, 3, wide, LANES), f32),
        ((4, groups1 // 2 + 1, 3, span, LANES), f32),
        ((ch * tr, LANES), f32),
    )
    return pl.pallas_call(
        functools.partial(decoder_kernel, tr, tc),
        out_shape=jax.ShapeDtypeStruct((ch, tr, tc), bf16),
        in_specs=[vm] * 6,
        out_specs=vm,
        scratch_shapes=[pltpu.VMEM(*s) for s in scratch],
        compiler_params=pltpu.CompilerParams(vmem_limit_bytes=DECODE_BYTES),
    )(terms, *packed)


def project_kernel(bins_hbm, row_hbm, col_hbm, send_ref, bins, w, sems):
    ch = row_hbm.shape[0]
    copies = [
        pltpu.make_async_copy(row_hbm, w.at[0:ch], sems.at[0]),
        pltpu.make_async_copy(col_hbm, w.at[LANES:LANES + ch], sems.at[1]),
        pltpu.make_async_copy(bins_hbm, bins, sems.at[2]),
    ]
    for copy in copies:
        copy.start()
    for p in range(2):
        w[p * LANES + ch:(p + 1) * LANES] = jnp.zeros((LANES - ch, w.shape[1]), w.dtype)
    for copy in copies:
        copy.wait()
    both = lax.dot_general(bins[...], w[...], NT, preferred_element_type=jnp.float32)
    both = both.astype(send_ref.dtype)
    for k in range(send_ref.shape[0]):
        send_ref[k] = both


def project(bins, row_proj, col_proj, peers):
    return pl.pallas_call(
        project_kernel,
        out_shape=jax.ShapeDtypeStruct((peers, bins.shape[0], 2 * LANES), jnp.bfloat16),
        in_specs=[pl.BlockSpec(memory_space=pltpu.HBM)] * 3,
        out_specs=pl.BlockSpec(memory_space=pltpu.VMEM),
        scratch_shapes=[
            pltpu.VMEM(bins.shape, bins.dtype),
            pltpu.VMEM((2 * LANES, bins.shape[1]), bins.dtype),
            pltpu.SemaphoreType.DMA((3,)),
        ],
    )(bins, row_proj, col_proj)


def shards(bins, row_proj, col_proj, conv_weight, conv_bias):
    rows = lax.axis_size("row")
    cols = lax.axis_size("col")
    reps = lax.axis_size("rep")
    part = conv_bias.shape[1]
    if reps > 1:
        row_proj = lax.all_gather(row_proj, "rep", axis=0, tiled=True)
        col_proj = lax.all_gather(col_proj, "rep", axis=0, tiled=True)
        conv_weight = lax.all_gather(conv_weight, "rep", axis=2, tiled=True)
        conv_bias = lax.all_gather(conv_bias, "rep", axis=1, tiled=True)
    peers = rows * cols
    total = bins.shape[0] * peers
    send = project(bins, row_proj, col_proj, peers)
    terms = lax.all_to_all(send, ("row", "col"), 0, 0, tiled=True)
    terms = terms.reshape(total, 2 * LANES)
    packed = filters(conv_weight, conv_bias)
    out = decode(terms, packed, total // rows, total // cols)
    if reps > 1:
        out = lax.dynamic_slice_in_dim(out, lax.axis_index("rep") * part, part, 0)
    return out


def solution(mesh):
    placed = (
        P(("groups", "row", "col"), None),
        P("rep", None),
        P("rep", None),
        P(None, None, "rep", None),
        P(None, "rep"),
    )
    return jax.shard_map(
        shards,
        mesh=mesh,
        in_specs=placed,
        out_specs=P("rep", ("groups", "row"), "col"),
        check_vma=False,
    )
```

time: 27.8 us -> 27.3 us (0.982)
  Pallas kernels: 12.2 us -> 10.8 us
  local copies, waits for them, and re-layouts: 1.77 us -> 2.52 us
    pallas_call x1, Pallas kernels: 9.58 us -> 7.91 us  [decode(): pl.pallas_call(functools.partial(decoder_kernel, tr, tc), out_shape=jax.S...]
    unnamed x4 -> x8, local copies, waits for them, and re-layouts: 1.77 us -> 2.52 us
  transfers between devices with their start and end apart: 1 -> 1, of which waited for: 1 -> 1; matrix products, arithmetic and copies ran while one was open for 0% -> 0% of each run, Pallas kernels for 2% -> 3%
where the time goes in v3:
time: 27.3 us; the launch traced here: 27 us
  Pallas kernels  10.8 us (40%)
  starting transfers between devices  7.33 us (27%)
  waiting for transfers between devices  6.36 us (23%)
  local copies, waits for them, and re-layouts  2.52 us (9%)
    pallas_call x1, Pallas kernels, decode(): pl.pallas_call(functools.partial(decoder_kernel, tr, tc), out_shape=jax.S...  7.91 us
    all_to_all x1, starting transfers between devices, shards(): terms = lax.all_to_all(send, ('row', 'col'), 0, 0, tiled=True)  7.33 us
    all_to_all x1, waiting for transfers between devices, shards(): terms = lax.all_to_all(send, ('row', 'col'), 0, 0, tiled=True)  6.36 us
    unnamed x8, local copies, waits for them, and re-layouts  2.52 us
    pallas_call x1, Pallas kernels, project(): pl.pallas_call(project_kernel, out_shape=jax.ShapeDtypeStruct((peers, bin...  2.12 us
    pallas_call x1, Pallas kernels, filters(): pl.pallas_call(filters_kernel, out_shape=[jax.ShapeDtypeStruct(*s) for s...  0.73 us
  transfers between devices with their start and end apart: 1, of which 1 were waited for; matrix products, arithmetic and copies ran while one was open for 0% of the time, Pallas kernels for 3%

profile of v3, /device:TPU:0, one launch (start us, length us, event | category | flops | bytes accessed | tf_op | source)
XLA Modules:
  0.0 27.0 jit_solution(2542569859707011403)
XLA Ops:
  0.0 0.0 copy-start
  0.0 2.1 %shard_map.55 = bf16[32,8,256]{2,1,0:T(8,128)(2,1)} custom-call(bf16[8,1536]{1,0:T(8,128)(2,1)} %bins_hbm.1, bf16[96,1536]{1,0:T(8,128)(2,1)} %row_hbm.1, bf16[96,1536]{1,0:T(8,128)(2,1)} %col_hbm.1), custom_call_target="tpu_custom_call" | custom-call | tf_op jit(solution)/shard_map/pallas_call | solution.py:291
  2.1 7.3 %all-to-all-start = ((bf16[32,8,256]{2,1,0:T(8,128)(2,1)}), bf16[32,8,256]{2,1,0:T(8,128)(2,1)S(1)}, u32[]{:S(2)}, u32[]{:S(2)}) async-start(bf16[32,8,256]{2,1,0:T(8,128)(2,1)} %shard_map.55), calls=%async_computation | async-start | bytes 262144 | tf_op jit(solution)/shard_map/all_to_all | solution.py:317
  9.5 0.0 copy-done
  9.5 0.0 copy-start.3
  9.5 0.7 %copy-done.3 = f32[3,96]{1,0:T(4,128)S(1)} copy-done((f32[3,96]{1,0:T(4,128)S(1)}, f32[3,96]{1,0:T(4,128)}, u32[]{:S(2)}) %copy-start.3) | copy-done | bytes 1176
  10.2 0.7 %shard_map.56 = (bf16[256,2304]{1,0:T(8,128)(2,1)S(1)}, bf16[256,2304]{1,0:T(8,128)(2,1)S(1)}, bf16[192,1408]{1,0:T(8,128)(2,1)S(1)}, f32[3,128]{1,0:T(4,128)S(1)}, f32[96,128]{1,0:T(8,128)S(1)}) custom-call(bf16[3,9,96,96]{3,2,1,0:T(8,128)(2,1)S(1)} %copy-done, f32[3,96]{1,0:T(4,128)S(1)} %copy-done.3), custom_call_target="tpu_custom_call" | custom-call | bytes 8388608 | tf_op jit(solution)/shard_map/pallas_call | solution.py:231
  10.9 0.0 copy-start.1
  10.9 0.8 %copy-done.1 = bf16[192,1408]{1,0:T(8,128)(2,1)} copy-done((bf16[192,1408]{1,0:T(8,128)(2,1)}, bf16[192,1408]{1,0:T(8,128)(2,1)S(1)}, u32[]{:S(2)}) %copy-start.1) | copy-done | bytes 540696
  11.7 6.4 %all-to-all-done = bf16[32,8,256]{2,1,0:T(8,128)(2,1)S(1)} async-done(((bf16[32,8,256]{2,1,0:T(8,128)(2,1)}), bf16[32,8,256]{2,1,0:T(8,128)(2,1)S(1)}, u32[]{:S(2)}, u32[]{:S(2)}) %all-to-all-start) | async-done | bytes 131104 | tf_op jit(solution)/shard_map/all_to_all | solution.py:317
  18.1 0.0 copy-start.2
  18.1 1.0 %copy-done.2 = bf16[192,1408]{1,0:T(8,128)(2,1)S(1)} copy-done((bf16[192,1408]{1,0:T(8,128)(2,1)S(1)}, bf16[192,1408]{1,0:T(8,128)(2,1)}, u32[]{:S(2)}) %copy-start.2) | copy-done | bytes 540696
  19.1 7.9 %shard_map.57 = bf16[96,16,128]{2,1,0:T(8,128)(2,1)} custom-call(bf16[256,256]{1,0:T(8,128)(2,1)S(1)} %bitcast.1, bf16[256,2304]{1,0:T(8,128)(2,1)S(1)} %get-tuple-element.10.packed0, bf16[256,2304]{1,0:T(8,128)(2,1)S(1)} %get-tuple-element.11.packed1, bf16[192,1408]{1,0:T(8,128)(2,1)S(1)} %copy-done.2, f32[3,128]{1,0:T(4,128)S(1)} %get-tuple-element.13.bias_ref, ...), custom_call_target="tpu_custom_call" | custom-call | tf_op jit(solution)/shard_map/pallas_call | solution.py:261
Async XLA Ops:
  0.0 9.5 %copy-start = (bf16[3,9,96,96]{3,2,1,0:T(8,128)(2,1)S(1)}, bf16[3,9,96,96]{3,2,1,0:T(8,128)(2,1)}, u32[]{:S(2)}) copy-start(bf16[3,9,96,96]{3,2,1,0:T(8,128)(2,1)} %w_ref.1) | copy-start | bytes 1492996
  2.1 15.9 %all-to-all-start = ((bf16[32,8,256]{2,1,0:T(8,128)(2,1)}), bf16[32,8,256]{2,1,0:T(8,128)(2,1)S(1)}, u32[]{:S(2)}, u32[]{:S(2)}) async-start(bf16[32,8,256]{2,1,0:T(8,128)(2,1)} %shard_map.55), calls=%async_computation | async-start | bytes 262144 | tf_op jit(solution)/shard_map/all_to_all | solution.py:317
  9.5 0.7 %copy-start.3 = (f32[3,96]{1,0:T(4,128)S(1)}, f32[3,96]{1,0:T(4,128)}, u32[]{:S(2)}) copy-start(f32[3,96]{1,0:T(4,128)} %b_ref.1) | copy-start | bytes 3460
  10.9 0.8 %copy-start.1 = (bf16[192,1408]{1,0:T(8,128)(2,1)}, bf16[192,1408]{1,0:T(8,128)(2,1)S(1)}, u32[]{:S(2)}) copy-start(bf16[192,1408]{1,0:T(8,128)(2,1)S(1)} %get-tuple-element.12.last) | copy-start | bytes 1622020
  18.1 1.0 %copy-start.2 = (bf16[192,1408]{1,0:T(8,128)(2,1)S(1)}, bf16[192,1408]{1,0:T(8,128)(2,1)}, u32[]{:S(2)}) copy-start(bf16[192,1408]{1,0:T(8,128)(2,1)} %copy-done.1) | copy-start | bytes 1622020

commit v4 on v3

--- a/solution.py
+++ b/solution.py
@@ -14,6 +14,8 @@
 STEP2 = 1
 APART = True
 WIDTH = BLOCKS * LANES
+LAST = 4 * WIDTH
+PACKED = LAST + WIDTH + 2 * LANES
 FRONT_BYTES = 48 << 20
 DECODE_BYTES = 40 << 20
 NT = (((1,), (1,)), ((), ()))
@@ -34,13 +36,13 @@
     return pltpu.roll(value, (ch - t * spare) % LANES, value.ndim - 1)
 
 
-def filters_kernel(w_ref, b_ref, packed0, packed1, last, bias_ref, column_ref, wide):
+def filters_kernel(w_ref, b_ref, packed, bias_ref, column_ref, wide):
     ch = w_ref.shape[2]
     spare = LANES - ch
     f32, bf16 = jnp.float32, jnp.bfloat16
     wide[...] = jnp.zeros(wide.shape, f32)
 
-    def fill(ref, rows0, rows1, first, layer, swap):
+    def fill(rows0, rows1, first, layer, swap):
         for b in range(3):
             taps = []
             for a in range(3):
@@ -48,26 +50,24 @@
                 taps.append(wide[...])
             for t in range(3):
                 cols = slice(first + (3 * t + b) * LANES, first + (3 * t + b + 1) * LANES)
-                ref[rows0, cols] = taps[t].astype(bf16)
+                packed[rows0, cols] = taps[t].astype(bf16)
                 main = taps[t - 1] if t else jnp.zeros((ch, LANES), f32)
                 moved = third_of(taps[2], ch, t)
-                ref[rows1, cols] = jnp.where(lane_ids((ch, LANES)) < ch, main, moved).astype(bf16)
+                packed[rows1, cols] = jnp.where(lane_ids((ch, LANES)) < ch, main, moved).astype(bf16)
 
     low, high = slice(0, ch), slice(LANES, LANES + ch)
-    for ref in (packed0, packed1):
-        for p in range(2):
-            ref[p * LANES + ch:(p + 1) * LANES] = jnp.zeros((spare, ref.shape[1]), bf16)
-    fill(packed0, low, high, 0, 0, False)
-    fill(packed0, low, high, WIDTH, 0, True)
-    fill(packed1, low, high, 0, 1, False)
-    fill(packed1, low, high, WIDTH, 1, True)
-    fill(last, slice(0, ch), slice(ch, 2 * ch), 0, 2, False)
+    for p in range(2):
+        packed[p * LANES + ch:(p + 1) * LANES, 0:LAST] = jnp.zeros((spare, LAST), bf16)
+    for layer in range(2):
+        fill(low, high, 2 * layer * WIDTH, layer, False)
+        fill(low, high, (2 * layer + 1) * WIDTH, layer, True)
+    fill(slice(0, ch), slice(ch, 2 * ch), LAST, 2, False)
     eye = lax.broadcasted_iota(jnp.int32, (ch, LANES), 0) == lane_ids((ch, LANES))
     unit = jnp.where(eye, 1.0, 0.0)
     for p in range(2):
         for s in range(2):
             part = unit if p == s else jnp.zeros((ch, LANES), f32)
-            last[p * ch:(p + 1) * ch, WIDTH + s * LANES:WIDTH + (s + 1) * LANES] = part.astype(bf16)
+            packed[p * ch:(p + 1) * ch, PACKED - (2 - s) * LANES:PACKED - (1 - s) * LANES] = part.astype(bf16)
     blank = jnp.zeros((b_ref.shape[0], spare), f32)
     bias = jnp.concatenate([b_ref[...], blank], axis=1)
     bias_ref[...] = bias
@@ -75,7 +75,7 @@
         jnp.sum(unit * bias[2:3, :], axis=1, keepdims=True), (ch, LANES))
 
 
-def decoder_kernel(tr, tc, terms_ref, packed0, packed1, last, bias_ref, column_ref, out_ref,
+def decoder_kernel(tr, tc, terms_ref, packed, bias_ref, column_ref, out_ref,
                    rows_f, cols_f, mixed_v, mixed_u, plain_v, plain_u, h1, sym, acc):
     bins = terms_ref.shape[0]
     ch = out_ref.shape[0]
@@ -159,7 +159,7 @@
                     v = mixed_v[m, t, b:b + wide, :].astype(bf16)
                     line.append(jnp.maximum(v * u, 0))
             rows.append(jnp.concatenate(line, axis=1))
-        y = lax.dot_general(jnp.concatenate(rows, axis=0), packed0[:, m * WIDTH:(m + 1) * WIDTH], NT,
+        y = lax.dot_general(jnp.concatenate(rows, axis=0), packed[:, m * WIDTH:(m + 1) * WIDTH], NT,
                             preferred_element_type=f32)
         for k, n in enumerate(range(lo, hi)):
             for e in range(2):
@@ -182,7 +182,7 @@
                     cut = jnp.concatenate([
                         h1[m, e, k + 1, t, 2 + 2 * b:2 + 2 * b + span, :] for k, e in spots], axis=0)
                     lhs.append(jnp.maximum(cut.astype(bf16), 0))
-        y = lax.dot_general(jnp.concatenate(lhs, axis=1), packed1[...], NT, preferred_element_type=f32)
+        y = lax.dot_general(jnp.concatenate(lhs, axis=1), packed[:, 2 * WIDTH:LAST], NT, preferred_element_type=f32)
         for s, (k, e) in enumerate(spots):
             for p in range(2):
                 both = h1[0, e, k + 1, 1 + p, 4:4 + span, :] + h1[1, e, k + 1, 1 + p, 4:4 + span, :]
@@ -206,7 +206,7 @@
             for p in range(2):
                 line.append(sym[e, g + 1, 1 + p, 4:4 + tc, :].astype(bf16))
             cells.append(jnp.concatenate(line, axis=1))
-        y = lax.dot_general(last[...], jnp.concatenate(cells, axis=0), NT, preferred_element_type=f32)
+        y = lax.dot_general(packed[0:2 * ch, LAST:PACKED], jnp.concatenate(cells, axis=0), NT, preferred_element_type=f32)
         for s, (g, e) in enumerate(spots):
             for p in range(2):
                 part = y[p * ch:(p + 1) * ch, s * tc:(s + 1) * tc]
@@ -222,9 +222,7 @@
     f32, bf16 = jnp.float32, jnp.bfloat16
     vm = pl.BlockSpec(memory_space=pltpu.VMEM)
     shapes = (
-        ((2 * LANES, 2 * WIDTH), bf16),
-        ((2 * LANES, 2 * WIDTH), bf16),
-        ((2 * ch, WIDTH + 2 * LANES), bf16),
+        ((2 * LANES, PACKED), bf16),
         ((bias.shape[0], LANES), f32),
         ((ch, LANES), f32),
     )
@@ -241,7 +239,7 @@
 
 def decode(terms, packed, tr, tc):
     bins = terms.shape[0]
-    ch = packed[4].shape[0]
+    ch = packed[2].shape[0]
     f32, bf16 = jnp.float32, jnp.bfloat16
     vm = pl.BlockSpec(memory_space=pltpu.VMEM)
     wide, span = tc + 16, tc + 8
@@ -261,7 +259,7 @@
     return pl.pallas_call(
         functools.partial(decoder_kernel, tr, tc),
         out_shape=jax.ShapeDtypeStruct((ch, tr, tc), bf16),
-        in_specs=[vm] * 6,
+        in_specs=[vm] * 4,
         out_specs=vm,
         scratch_shapes=[pltpu.VMEM(*s) for s in scratch],
         compiler_params=pltpu.CompilerParams(vmem_limit_bytes=DECODE_BYTES),

time: 27.3 us -> 26.2 us (0.960)
  local copies, waits for them, and re-layouts: 2.52 us -> 1.77 us
    unnamed x8 -> x4, local copies, waits for them, and re-layouts: 2.52 us -> 1.77 us
where the time goes in v4:
time: 26.2 us; the launch traced here: 25.9 us
  Pallas kernels  10.7 us (41%)
  starting transfers between devices  7.33 us (28%)
  waiting for transfers between devices  6.09 us (23%)
  local copies, waits for them, and re-layouts  1.77 us (7%)
    pallas_call x1, Pallas kernels, decode(): pl.pallas_call(functools.partial(decoder_kernel, tr, tc), out_shape=jax.S...  7.94 us
    all_to_all x1, starting transfers between devices, shards(): terms = lax.all_to_all(send, ('row', 'col'), 0, 0, tiled=True)  7.33 us
    all_to_all x1, waiting for transfers between devices, shards(): terms = lax.all_to_all(send, ('row', 'col'), 0, 0, tiled=True)  6.09 us
    pallas_call x1, Pallas kernels, project(): pl.pallas_call(project_kernel, out_shape=jax.ShapeDtypeStruct((peers, bin...  2.06 us
    unnamed x4, local copies, waits for them, and re-layouts  1.77 us
    pallas_call x1, Pallas kernels, filters(): pl.pallas_call(filters_kernel, out_shape=[jax.ShapeDtypeStruct(*s) for s...  0.73 us
  transfers between devices with their start and end apart: 1, of which 1 were waited for; matrix products, arithmetic and copies ran while one was open for 0% of the time, Pallas kernels for 3%

profile of v4, /device:TPU:0, one launch (start us, length us, event | category | flops | bytes accessed | tf_op | source)
XLA Modules:
  0.0 25.9 jit_solution(17631348423234030845)
XLA Ops:
  0.0 2.1 %shard_map.55 = bf16[32,8,256]{2,1,0:T(8,128)(2,1)} custom-call(bf16[8,1536]{1,0:T(8,128)(2,1)} %bins_hbm.1, bf16[96,1536]{1,0:T(8,128)(2,1)} %row_hbm.1, bf16[96,1536]{1,0:T(8,128)(2,1)} %col_hbm.1), custom_call_target="tpu_custom_call" | custom-call | tf_op jit(solution)/shard_map/pallas_call | solution.py:289
  2.1 7.3 %all-to-all-start = ((bf16[32,8,256]{2,1,0:T(8,128)(2,1)}), bf16[32,8,256]{2,1,0:T(8,128)(2,1)S(1)}, u32[]{:S(2)}, u32[]{:S(2)}) async-start(bf16[32,8,256]{2,1,0:T(8,128)(2,1)} %shard_map.55), calls=%async_computation | async-start | bytes 262144 | tf_op jit(solution)/shard_map/all_to_all | solution.py:315
  9.4 0.0 copy-start
  9.4 1.1 %copy-done = bf16[3,9,96,96]{3,2,1,0:T(8,128)(2,1)S(1)} copy-done((bf16[3,9,96,96]{3,2,1,0:T(8,128)(2,1)S(1)}, bf16[3,9,96,96]{3,2,1,0:T(8,128)(2,1)}, u32[]{:S(2)}) %copy-start) | copy-done | bytes 497688
  10.5 0.0 copy-start.1
  10.5 0.7 %copy-done.1 = f32[3,96]{1,0:T(4,128)S(1)} copy-done((f32[3,96]{1,0:T(4,128)S(1)}, f32[3,96]{1,0:T(4,128)}, u32[]{:S(2)}) %copy-start.1) | copy-done | bytes 1176
  11.2 0.7 %shard_map.56 = (bf16[256,6016]{1,0:T(8,128)(2,1)S(1)}, f32[3,128]{1,0:T(4,128)S(1)}, f32[96,128]{1,0:T(8,128)S(1)}) custom-call(bf16[3,9,96,96]{3,2,1,0:T(8,128)(2,1)S(1)} %copy-done, f32[3,96]{1,0:T(4,128)S(1)} %copy-done.1), custom_call_target="tpu_custom_call" | custom-call | bytes 8388608 | tf_op jit(solution)/shard_map/pallas_call | solution.py:229
  11.9 6.1 %all-to-all-done = bf16[32,8,256]{2,1,0:T(8,128)(2,1)S(1)} async-done(((bf16[32,8,256]{2,1,0:T(8,128)(2,1)}), bf16[32,8,256]{2,1,0:T(8,128)(2,1)S(1)}, u32[]{:S(2)}, u32[]{:S(2)}) %all-to-all-start) | async-done | bytes 131104 | tf_op jit(solution)/shard_map/all_to_all | solution.py:315
  18.0 7.9 %shard_map.57 = bf16[96,16,128]{2,1,0:T(8,128)(2,1)} custom-call(bf16[256,256]{1,0:T(8,128)(2,1)S(1)} %bitcast.1, bf16[256,6016]{1,0:T(8,128)(2,1)S(1)} %get-tuple-element.8.packed, f32[3,128]{1,0:T(4,128)S(1)} %get-tuple-element.9.bias_ref, f32[96,128]{1,0:T(8,128)S(1)} %get-tuple-element.10.column_ref), custom_call_target="tpu_custom_call" | custom-call | tf_op jit(solution)/shard_map/pallas_call | solution.py:259
Async XLA Ops:
  2.1 15.9 %all-to-all-start = ((bf16[32,8,256]{2,1,0:T(8,128)(2,1)}), bf16[32,8,256]{2,1,0:T(8,128)(2,1)S(1)}, u32[]{:S(2)}, u32[]{:S(2)}) async-start(bf16[32,8,256]{2,1,0:T(8,128)(2,1)} %shard_map.55), calls=%async_computation | async-start | bytes 262144 | tf_op jit(solution)/shard_map/all_to_all | solution.py:315
  9.4 1.1 %copy-start = (bf16[3,9,96,96]{3,2,1,0:T(8,128)(2,1)S(1)}, bf16[3,9,96,96]{3,2,1,0:T(8,128)(2,1)}, u32[]{:S(2)}) copy-start(bf16[3,9,96,96]{3,2,1,0:T(8,128)(2,1)} %w_ref.1) | copy-start | bytes 1492996
  10.5 0.7 %copy-start.1 = (f32[3,96]{1,0:T(4,128)S(1)}, f32[3,96]{1,0:T(4,128)}, u32[]{:S(2)}) copy-start(f32[3,96]{1,0:T(4,128)} %b_ref.1) | copy-start | bytes 3460

commit v5 on v4

--- a/solution.py
+++ b/solution.py
@@ -77,7 +77,7 @@
 
 def decoder_kernel(tr, tc, terms_ref, packed, bias_ref, column_ref, out_ref,
                    rows_f, cols_f, mixed_v, mixed_u, plain_v, plain_u, h1, sym, acc):
-    bins = terms_ref.shape[0]
+    bins = terms_ref.shape[0] * terms_ref.shape[2] * 2
     ch = out_ref.shape[0]
     wide = tc + 16
     span = tc + 8
@@ -95,10 +95,23 @@
         else:
             body()
 
-    for tab, lo in ((rows_f, 0), (cols_f, LANES)):
+    peers, _, half, _ = terms_ref.shape
+    for tab in (rows_f, cols_f):
         tab[0:PAD] = jnp.zeros((PAD, LANES), f32)
         tab[PAD + bins:] = jnp.zeros((PAD, LANES), f32)
-        tab[PAD:PAD + bins] = terms_ref[:, lo:lo + LANES].astype(f32)
+    for s in range(peers):
+        rest = terms_ref[s, 2].astype(f32)
+        for i in range(2):
+            at = PAD + (2 * s + i) * half
+            rows_f[at:at + half] = terms_ref[s, i].astype(f32)
+            cols_f[at:at + half] = rest
+    spare = LANES - ch
+    shape = (bins, LANES)
+    rest = cols_f[PAD:PAD + bins]
+    early = lax.rem(lax.broadcasted_iota(jnp.int32, shape, 0), 2 * half) < half
+    rest = jnp.where(early, pltpu.roll(rest, spare, 1), pltpu.roll(rest, ch, 1))
+    cols_f[PAD:PAD + bins] = jnp.where(
+        lane_ids(shape) < spare, pltpu.roll(rows_f[PAD:PAD + bins], spare, 1), rest)
 
     pairs0 = (tr + 12) // 2
     tall = mixed_u.shape[2]
@@ -238,7 +251,7 @@
 
 
 def decode(terms, packed, tr, tc):
-    bins = terms.shape[0]
+    bins = terms.shape[0] * terms.shape[2] * 2
     ch = packed[2].shape[0]
     f32, bf16 = jnp.float32, jnp.bfloat16
     vm = pl.BlockSpec(memory_space=pltpu.VMEM)
@@ -268,32 +281,35 @@
 
 def project_kernel(bins_hbm, row_hbm, col_hbm, send_ref, bins, w, sems):
     ch = row_hbm.shape[0]
+    half = bins.shape[0] // 2
     copies = [
-        pltpu.make_async_copy(row_hbm, w.at[0:ch], sems.at[0]),
-        pltpu.make_async_copy(col_hbm, w.at[LANES:LANES + ch], sems.at[1]),
-        pltpu.make_async_copy(bins_hbm, bins, sems.at[2]),
+        pltpu.make_async_copy(bins_hbm, bins, sems.at[0]),
+        pltpu.make_async_copy(row_hbm, w.at[0:ch], sems.at[1]),
+        pltpu.make_async_copy(col_hbm, w.at[ch:2 * ch], sems.at[2]),
     ]
     for copy in copies:
         copy.start()
-    for p in range(2):
-        w[p * LANES + ch:(p + 1) * LANES] = jnp.zeros((LANES - ch, w.shape[1]), w.dtype)
     for copy in copies:
         copy.wait()
     both = lax.dot_general(bins[...], w[...], NT, preferred_element_type=jnp.float32)
-    both = both.astype(send_ref.dtype)
-    for k in range(send_ref.shape[0]):
-        send_ref[k] = both
+    full, rest = both[:, 0:LANES], both[:, LANES:]
+    rest = jnp.concatenate([rest[0:half], rest[half:]], axis=1)
+    for i, part in enumerate((full[0:half], full[half:], rest)):
+        part = part.astype(send_ref.dtype)
+        for k in range(send_ref.shape[0]):
+            send_ref[k, i] = part
 
 
 def project(bins, row_proj, col_proj, peers):
+    span = bins.shape[0]
     return pl.pallas_call(
         project_kernel,
-        out_shape=jax.ShapeDtypeStruct((peers, bins.shape[0], 2 * LANES), jnp.bfloat16),
+        out_shape=jax.ShapeDtypeStruct((peers, 3, span // 2, LANES), jnp.bfloat16),
         in_specs=[pl.BlockSpec(memory_space=pltpu.HBM)] * 3,
         out_specs=pl.BlockSpec(memory_space=pltpu.VMEM),
         scratch_shapes=[
             pltpu.VMEM(bins.shape, bins.dtype),
-            pltpu.VMEM((2 * LANES, bins.shape[1]), bins.dtype),
+            pltpu.VMEM((2 * row_proj.shape[0], bins.shape[1]), bins.dtype),
             pltpu.SemaphoreType.DMA((3,)),
         ],
     )(bins, row_proj, col_proj)
@@ -313,7 +329,6 @@
     total = bins.shape[0] * peers
     send = project(bins, row_proj, col_proj, peers)
     terms = lax.all_to_all(send, ("row", "col"), 0, 0, tiled=True)
-    terms = terms.reshape(total, 2 * LANES)
     packed = filters(conv_weight, conv_bias)
     out = decode(terms, packed, total // rows, total // cols)
     if reps > 1:

time: 26.2 us -> 25.8 us (0.985)
  waiting for transfers between devices: 6.09 us -> 5.57 us
    all_to_all x1, waiting for transfers between devices: 6.09 us -> 5.57 us  [shards(): terms = lax.all_to_all(send, ('row', 'col'), 0, 0, tiled=True)]
where the time goes in v5:
time: 25.8 us; the launch traced here: 25.6 us
  Pallas kernels  10.9 us (42%)
  starting transfers between devices  7.33 us (28%)
  waiting for transfers between devices  5.57 us (22%)
  local copies, waits for them, and re-layouts  1.77 us (7%)
    pallas_call x1, Pallas kernels, decode(): pl.pallas_call(functools.partial(decoder_kernel, tr, tc), out_shape=jax.S...  8.06 us
    all_to_all x1, starting transfers between devices, shards(): terms = lax.all_to_all(send, ('row', 'col'), 0, 0, tiled=True)  7.33 us
    all_to_all x1, waiting for transfers between devices, shards(): terms = lax.all_to_all(send, ('row', 'col'), 0, 0, tiled=True)  5.57 us
    pallas_call x1, Pallas kernels, project(): pl.pallas_call(project_kernel, out_shape=jax.ShapeDtypeStruct((peers, 3,...  2.08 us
    unnamed x4, local copies, waits for them, and re-layouts  1.77 us
    pallas_call x1, Pallas kernels, filters(): pl.pallas_call(filters_kernel, out_shape=[jax.ShapeDtypeStruct(*s) for s...  0.73 us
  transfers between devices with their start and end apart: 1, of which 1 were waited for; matrix products, arithmetic and copies ran while one was open for 0% of the time, Pallas kernels for 3%

profile of v5, /device:TPU:0, one launch (start us, length us, event | category | flops | bytes accessed | tf_op | source)
XLA Modules:
  0.0 25.6 jit_solution(2580984177889813789)
XLA Ops:
  0.0 2.1 %shard_map.55 = bf16[32,3,4,128]{3,2,1,0:T(4,128)(2,1)} custom-call(bf16[8,1536]{1,0:T(8,128)(2,1)} %bins_hbm.1, bf16[96,1536]{1,0:T(8,128)(2,1)} %row_hbm.1, bf16[96,1536]{1,0:T(8,128)(2,1)} %col_hbm.1), custom_call_target="tpu_custom_call" | custom-call | tf_op jit(solution)/shard_map/pallas_call | solution.py:305
  2.1 7.3 %all-to-all-start = ((bf16[32,3,4,128]{3,2,1,0:T(4,128)(2,1)}), bf16[32,3,4,128]{3,2,1,0:T(4,128)(2,1)S(1)}, u32[]{:S(2)}, u32[]{:S(2)}) async-start(bf16[32,3,4,128]{3,2,1,0:T(4,128)(2,1)} %shard_map.55), calls=%async_computation | async-start | bytes 196608 | tf_op jit(solution)/shard_map/all_to_all | solution.py:331
  9.4 0.0 copy-start
  9.4 1.1 %copy-done = bf16[3,9,96,96]{3,2,1,0:T(8,128)(2,1)S(1)} copy-done((bf16[3,9,96,96]{3,2,1,0:T(8,128)(2,1)S(1)}, bf16[3,9,96,96]{3,2,1,0:T(8,128)(2,1)}, u32[]{:S(2)}) %copy-start) | copy-done | bytes 497688
  10.5 0.0 copy-start.1
  10.5 0.7 %copy-done.1 = f32[3,96]{1,0:T(4,128)S(1)} copy-done((f32[3,96]{1,0:T(4,128)S(1)}, f32[3,96]{1,0:T(4,128)}, u32[]{:S(2)}) %copy-start.1) | copy-done | bytes 1176
  11.2 0.7 %shard_map.56 = (bf16[256,6016]{1,0:T(8,128)(2,1)S(1)}, f32[3,128]{1,0:T(4,128)S(1)}, f32[96,128]{1,0:T(8,128)S(1)}) custom-call(bf16[3,9,96,96]{3,2,1,0:T(8,128)(2,1)S(1)} %copy-done, f32[3,96]{1,0:T(4,128)S(1)} %copy-done.1), custom_call_target="tpu_custom_call" | custom-call | bytes 8388608 | tf_op jit(solution)/shard_map/pallas_call | solution.py:242
  11.9 5.6 %all-to-all-done.terms_ref = bf16[32,3,4,128]{3,2,1,0:T(4,128)(2,1)S(1)} async-done(((bf16[32,3,4,128]{3,2,1,0:T(4,128)(2,1)}), bf16[32,3,4,128]{3,2,1,0:T(4,128)(2,1)S(1)}, u32[]{:S(2)}, u32[]{:S(2)}) %all-to-all-start) | async-done | bytes 98336 | tf_op jit(solution)/shard_map/all_to_all | solution.py:331
  17.5 8.1 %shard_map.57 = bf16[96,16,128]{2,1,0:T(8,128)(2,1)} custom-call(bf16[32,3,4,128]{3,2,1,0:T(4,128)(2,1)S(1)} %all-to-all-done.terms_ref, bf16[256,6016]{1,0:T(8,128)(2,1)S(1)} %get-tuple-element.8.packed, f32[3,128]{1,0:T(4,128)S(1)} %get-tuple-element.9.bias_ref, f32[96,128]{1,0:T(8,128)S(1)} %get-tuple-element.10.column_ref), custom_call_target="tpu_custom_call" | custom-call | tf_op jit(solution)/shard_map/pallas_call | solution.py:272
Async XLA Ops:
  2.1 15.4 %all-to-all-start = ((bf16[32,3,4,128]{3,2,1,0:T(4,128)(2,1)}), bf16[32,3,4,128]{3,2,1,0:T(4,128)(2,1)S(1)}, u32[]{:S(2)}, u32[]{:S(2)}) async-start(bf16[32,3,4,128]{3,2,1,0:T(4,128)(2,1)} %shard_map.55), calls=%async_computation | async-start | bytes 196608 | tf_op jit(solution)/shard_map/all_to_all | solution.py:331
  9.4 1.1 %copy-start = (bf16[3,9,96,96]{3,2,1,0:T(8,128)(2,1)S(1)}, bf16[3,9,96,96]{3,2,1,0:T(8,128)(2,1)}, u32[]{:S(2)}) copy-start(bf16[3,9,96,96]{3,2,1,0:T(8,128)(2,1)} %w_ref.1) | copy-start | bytes 1492996
  10.5 0.7 %copy-start.1 = (f32[3,96]{1,0:T(4,128)S(1)}, f32[3,96]{1,0:T(4,128)}, u32[]{:S(2)}) copy-start(f32[3,96]{1,0:T(4,128)} %b_ref.1) | copy-start | bytes 3460

commit v6 on v5

--- a/solution.py
+++ b/solution.py
@@ -139,28 +139,23 @@
             for t in range(3):
                 ref[where + (at - 1, t, cells, slice(ch, LANES))] = third_of(value, ch, t)[:, ch:LANES]
 
-    def clear(ref, heads, groups, width, side, deep):
-        main, rest = slice(0, ch), slice(ch, LANES)
-        body = jnp.zeros((width, ch), f32)
-        tail = jnp.zeros((width, LANES - ch), f32)
-        edge = jnp.zeros((side, LANES), f32)
-        above = [(1, 0, main)] + ([(1, 1, main), (2, 0, main), (1, 2, main)] if deep == 3 else [])
-        below = [(groups, t, rest) for t in range(3)]
-        if deep == 3:
-            below += [(groups, 1, main), (groups, 2, main)] + [(groups - 1, t, rest) for t in range(3)]
-        for flag, places in ((top, above), (bottom, below)):
-            @pl.when(flag)
-            def _(places=places):
-                for head in heads:
-                    for at, t, lanes in places:
-                        ref[head + (at, t, slice(0, width), lanes)] = body if lanes == main else tail
-        for flag, start in ((left, 0), (right, width - side)):
-            @pl.when(flag)
-            def _(start=start):
-                for head in heads:
-                    for at in range(1, groups + 1):
-                        for t in range(3):
-                            ref[head + (at, t, slice(start, start + side), slice(0, LANES))] = edge
+    def kept(outside):
+        return jnp.where(outside, 0.0, 1.0).astype(f32)
+
+    keep_top, keep_bottom = kept(top), kept(bottom)
+    sub = lax.broadcasted_iota(jnp.int32, (8, LANES), 0)
+    sides0 = (jnp.full((8, LANES), kept(left)), jnp.full((8, LANES), kept(right)))
+    sides1 = (jnp.where((sub < 4) & left, 0.0, 1.0), jnp.where((sub >= 4) & right, 0.0, 1.0))
+
+    def inside(value, sides, above, below):
+        width = value.shape[0]
+        value = jnp.concatenate([
+            value[0:8] * sides[0], value[8:width - 8], value[width - 8:] * sides[1]], axis=0)
+        if above:
+            value = value * keep_top
+        if below:
+            value = value * keep_bottom
+        return value
 
     def first(m, lo, hi):
         rows = []
@@ -178,13 +173,13 @@
             for e in range(2):
                 own = plain_v[m, 1:1 + wide, :] * plain_u[m, 2 * n + e:2 * n + e + 1, :]
                 part = y[k * wide:(k + 1) * wide, e * LANES:(e + 1) * LANES]
-                put(h1, (m, e), n, part + own + bias0, wide)
+                value = inside(part + own + bias0, sides0, n < 3, n >= pairs0 - 3)
+                put(h1, (m, e), n, value, wide)
 
     for m in range(2):
         for lo, hi in cuts(pairs0, STEP0):
             stage(functools.partial(first, m, lo, hi))
     groups1 = (tr + 8) // 4
-    clear(h1, [(m, e) for m in range(2) for e in range(2)], groups1, wide, 8, 3)
 
     def second(lo, hi):
         spots = [(k, e) for k in range(lo, hi) for e in range(2)]
@@ -200,12 +195,12 @@
             for p in range(2):
                 both = h1[0, e, k + 1, 1 + p, 4:4 + span, :] + h1[1, e, k + 1, 1 + p, 4:4 + span, :]
                 part = y[s * span:(s + 1) * span, p * LANES:(p + 1) * LANES]
-                put(sym, (e + 2 * p,), k, (part + both) * 0.5 + bias1, span)
+                value = inside((part + both) * 0.5 + bias1, sides1, k < 1, k >= groups1 - 1)
+                put(sym, (e + 2 * p,), k, value, span)
 
     for lo, hi in cuts(groups1, STEP1):
         stage(functools.partial(second, lo, hi))
     groups2 = tr // 8
-    clear(sym, [(e,) for e in range(4)], groups2, span, 4, 1)
 
     bias2 = column_ref[...]
     def third(lo, hi):

time: 25.8 us -> 25.3 us (0.981)
  Pallas kernels: 10.9 us -> 10.4 us
    pallas_call x1, Pallas kernels: 8.06 us -> 7.57 us  [decode(): pl.pallas_call(functools.partial(decoder_kernel, tr, tc), out_shape=jax.S...]
where the time goes in v6:
time: 25.3 us; the launch traced here: 25.1 us
  Pallas kernels  10.4 us (41%)
  starting transfers between devices  7.33 us (29%)
  waiting for transfers between devices  5.57 us (22%)
  local copies, waits for them, and re-layouts  1.77 us (7%)
    pallas_call x1, Pallas kernels, decode(): pl.pallas_call(functools.partial(decoder_kernel, tr, tc), out_shape=jax.S...  7.57 us
    all_to_all x1, starting transfers between devices, shards(): terms = lax.all_to_all(send, ('row', 'col'), 0, 0, tiled=True)  7.33 us
    all_to_all x1, waiting for transfers between devices, shards(): terms = lax.all_to_all(send, ('row', 'col'), 0, 0, tiled=True)  5.57 us
    pallas_call x1, Pallas kernels, project(): pl.pallas_call(project_kernel, out_shape=jax.ShapeDtypeStruct((peers, 3,...  2.08 us
    unnamed x4, local copies, waits for them, and re-layouts  1.77 us
    pallas_call x1, Pallas kernels, filters(): pl.pallas_call(filters_kernel, out_shape=[jax.ShapeDtypeStruct(*s) for s...  0.73 us
  transfers between devices with their start and end apart: 1, of which 1 were waited for; matrix products, arithmetic and copies ran while one was open for 0% of the time, Pallas kernels for 3%

profile of v6, /device:TPU:0, one launch (start us, length us, event | category | flops | bytes accessed | tf_op | source)
XLA Modules:
  0.0 25.1 jit_solution(12237393179642707592)
XLA Ops:
  0.0 2.1 %shard_map.55 = bf16[32,3,4,128]{3,2,1,0:T(4,128)(2,1)} custom-call(bf16[8,1536]{1,0:T(8,128)(2,1)} %bins_hbm.1, bf16[96,1536]{1,0:T(8,128)(2,1)} %row_hbm.1, bf16[96,1536]{1,0:T(8,128)(2,1)} %col_hbm.1), custom_call_target="tpu_custom_call" | custom-call | tf_op jit(solution)/shard_map/pallas_call | solution.py:300
  2.1 7.3 %all-to-all-start = ((bf16[32,3,4,128]{3,2,1,0:T(4,128)(2,1)}), bf16[32,3,4,128]{3,2,1,0:T(4,128)(2,1)S(1)}, u32[]{:S(2)}, u32[]{:S(2)}) async-start(bf16[32,3,4,128]{3,2,1,0:T(4,128)(2,1)} %shard_map.55), calls=%async_computation | async-start | bytes 196608 | tf_op jit(solution)/shard_map/all_to_all | solution.py:326
  9.4 0.0 copy-start
  9.4 1.1 %copy-done = bf16[3,9,96,96]{3,2,1,0:T(8,128)(2,1)S(1)} copy-done((bf16[3,9,96,96]{3,2,1,0:T(8,128)(2,1)S(1)}, bf16[3,9,96,96]{3,2,1,0:T(8,128)(2,1)}, u32[]{:S(2)}) %copy-start) | copy-done | bytes 497688
  10.5 0.0 copy-start.1
  10.5 0.7 %copy-done.1 = f32[3,96]{1,0:T(4,128)S(1)} copy-done((f32[3,96]{1,0:T(4,128)S(1)}, f32[3,96]{1,0:T(4,128)}, u32[]{:S(2)}) %copy-start.1) | copy-done | bytes 1176
  11.2 0.7 %shard_map.56 = (bf16[256,6016]{1,0:T(8,128)(2,1)S(1)}, f32[3,128]{1,0:T(4,128)S(1)}, f32[96,128]{1,0:T(8,128)S(1)}) custom-call(bf16[3,9,96,96]{3,2,1,0:T(8,128)(2,1)S(1)} %copy-done, f32[3,96]{1,0:T(4,128)S(1)} %copy-done.1), custom_call_target="tpu_custom_call" | custom-call | bytes 8388608 | tf_op jit(solution)/shard_map/pallas_call | solution.py:237
  11.9 5.6 %all-to-all-done.terms_ref = bf16[32,3,4,128]{3,2,1,0:T(4,128)(2,1)S(1)} async-done(((bf16[32,3,4,128]{3,2,1,0:T(4,128)(2,1)}), bf16[32,3,4,128]{3,2,1,0:T(4,128)(2,1)S(1)}, u32[]{:S(2)}, u32[]{:S(2)}) %all-to-all-start) | async-done | bytes 98336 | tf_op jit(solution)/shard_map/all_to_all | solution.py:326
  17.5 7.6 %shard_map.57 = bf16[96,16,128]{2,1,0:T(8,128)(2,1)} custom-call(bf16[32,3,4,128]{3,2,1,0:T(4,128)(2,1)S(1)} %all-to-all-done.terms_ref, bf16[256,6016]{1,0:T(8,128)(2,1)S(1)} %get-tuple-element.8.packed, f32[3,128]{1,0:T(4,128)S(1)} %get-tuple-element.9.bias_ref, f32[96,128]{1,0:T(8,128)S(1)} %get-tuple-element.10.column_ref), custom_call_target="tpu_custom_call" | custom-call | tf_op jit(solution)/shard_map/pallas_call | solution.py:267
Async XLA Ops:
  2.1 15.4 %all-to-all-start = ((bf16[32,3,4,128]{3,2,1,0:T(4,128)(2,1)}), bf16[32,3,4,128]{3,2,1,0:T(4,128)(2,1)S(1)}, u32[]{:S(2)}, u32[]{:S(2)}) async-start(bf16[32,3,4,128]{3,2,1,0:T(4,128)(2,1)} %shard_map.55), calls=%async_computation | async-start | bytes 196608 | tf_op jit(solution)/shard_map/all_to_all | solution.py:326
  9.4 1.1 %copy-start = (bf16[3,9,96,96]{3,2,1,0:T(8,128)(2,1)S(1)}, bf16[3,9,96,96]{3,2,1,0:T(8,128)(2,1)}, u32[]{:S(2)}) copy-start(bf16[3,9,96,96]{3,2,1,0:T(8,128)(2,1)} %w_ref.1) | copy-start | bytes 1492996
  10.5 0.7 %copy-start.1 = (f32[3,96]{1,0:T(4,128)S(1)}, f32[3,96]{1,0:T(4,128)}, u32[]{:S(2)}) copy-start(f32[3,96]{1,0:T(4,128)} %b_ref.1) | copy-start | bytes 3460

commit v7 on v6

--- a/solution.py
+++ b/solution.py
@@ -9,10 +9,11 @@
 LANES = 128
 PAD = 16
 BLOCKS = 9
-STEP0 = 4
-STEP1 = 1
-STEP2 = 1
+STEP0 = 7
+STEP1 = 3
 APART = True
+BESIDE = True
+MIXED = False
 WIDTH = BLOCKS * LANES
 LAST = 4 * WIDTH
 PACKED = LAST + WIDTH + 2 * LANES
@@ -91,7 +92,7 @@
 
     def stage(body):
         if APART:
-            pl.when(i0 >= 0)(body)
+            pl.when(i0 < bins)(body)
         else:
             body()
 
@@ -105,28 +106,37 @@
             at = PAD + (2 * s + i) * half
             rows_f[at:at + half] = terms_ref[s, i].astype(f32)
             cols_f[at:at + half] = rest
-    spare = LANES - ch
-    shape = (bins, LANES)
-    rest = cols_f[PAD:PAD + bins]
-    early = lax.rem(lax.broadcasted_iota(jnp.int32, shape, 0), 2 * half) < half
-    rest = jnp.where(early, pltpu.roll(rest, spare, 1), pltpu.roll(rest, ch, 1))
-    cols_f[PAD:PAD + bins] = jnp.where(
-        lane_ids(shape) < spare, pltpu.roll(rows_f[PAD:PAD + bins], spare, 1), rest)
+
+    def row_terms(at, count, phase):
+        first = rows_f[pl.ds(at, count), :]
+        return first, lambda: [third_of(first, ch, t) for t in range(3)]
+
+    def col_terms(at, count, phase):
+        first, rest = rows_f[pl.ds(at, count), :], cols_f[pl.ds(at, count), :]
+        shape = (count, LANES)
+        early = lax.rem(lax.broadcasted_iota(jnp.int32, shape, 0) + phase, 2 * half) < half
+        spare = LANES - ch
+        one, three = pltpu.roll(rest, spare, 1), pltpu.roll(rest, ch, 1)
+        main = jnp.where(early, one, three)
+        main = jnp.where(lane_ids(shape) < spare, pltpu.roll(first, spare, 1), main)
+        return main, lambda: [
+            first, jnp.where(early, three, one), jnp.where(early, pltpu.roll(rest, 2 * spare, 1), rest)]
 
     pairs0 = (tr + 12) // 2
     tall = mixed_u.shape[2]
     body_v = lane_ids((wide + 8, LANES)) < ch
     body_u = lane_ids((tall, LANES)) < ch
-    for m, (u_src, v_src) in enumerate(((rows_f, cols_f), (cols_f, rows_f))):
-        line = v_src[pl.ds(j0 + PAD - 9, wide + 8), :]
+    for m, (u_terms, v_terms) in enumerate(((row_terms, col_terms), (col_terms, row_terms))):
+        _, fourth = u_terms(i0 + PAD - 4, tall, PAD - 4)
+        for t, moved in enumerate(fourth()):
+            row, _ = u_terms(i0 + PAD - 7 + t, tall, PAD - 7 + t)
+            mixed_u[m, t] = jnp.where(body_u, row, moved)
+            if t == 1:
+                plain_u[m] = row
+        line, parts = v_terms(j0 + PAD - 9, wide + 8, PAD - 9)
         plain_v[m] = line
-        for t in range(3):
-            mixed_v[m, t] = jnp.where(body_v, line, third_of(line, ch, t))
-        fourth = u_src[pl.ds(i0 + PAD - 7 + 3, tall), :]
-        for t in range(3):
-            row = u_src[pl.ds(i0 + PAD - 7 + t, tall), :]
-            mixed_u[m, t] = jnp.where(body_u, row, third_of(fourth, ch, t))
-        plain_u[m] = u_src[pl.ds(i0 + PAD - 6, tall), :]
+        for t, moved in enumerate(parts()):
+            mixed_v[m, t] = jnp.where(body_v, line, moved)
 
     def put(ref, where, k, value, width):
         at = k // 2 + 1
@@ -176,9 +186,11 @@
                 value = inside(part + own + bias0, sides0, n < 3, n >= pairs0 - 3)
                 put(h1, (m, e), n, value, wide)
 
-    for m in range(2):
-        for lo, hi in cuts(pairs0, STEP0):
-            stage(functools.partial(first, m, lo, hi))
+    order = [(m, lo, hi) for lo, hi in cuts(pairs0, STEP0) for m in range(2)]
+    if not MIXED:
+        order = sorted(order)
+    for m, lo, hi in order:
+        stage(functools.partial(first, m, lo, hi))
     groups1 = (tr + 8) // 4
 
     def second(lo, hi):
@@ -190,23 +202,24 @@
                     cut = jnp.concatenate([
                         h1[m, e, k + 1, t, 2 + 2 * b:2 + 2 * b + span, :] for k, e in spots], axis=0)
                     lhs.append(jnp.maximum(cut.astype(bf16), 0))
-        y = lax.dot_general(jnp.concatenate(lhs, axis=1), packed[:, 2 * WIDTH:LAST], NT, preferred_element_type=f32)
-        for s, (k, e) in enumerate(spots):
-            for p in range(2):
-                both = h1[0, e, k + 1, 1 + p, 4:4 + span, :] + h1[1, e, k + 1, 1 + p, 4:4 + span, :]
-                part = y[s * span:(s + 1) * span, p * LANES:(p + 1) * LANES]
-                value = inside((part + both) * 0.5 + bias1, sides1, k < 1, k >= groups1 - 1)
-                put(sym, (e + 2 * p,), k, value, span)
-
-    for lo, hi in cuts(groups1, STEP1):
-        stage(functools.partial(second, lo, hi))
+        y = lax.dot_general(jnp.concatenate(lhs, axis=1), packed[:, 2 * WIDTH:LAST], NT,
+                            preferred_element_type=f32)
+
+        def finish():
+            for s, (k, e) in enumerate(spots):
+                for p in range(2):
+                    both = h1[0, e, k + 1, 1 + p, 4:4 + span, :] + h1[1, e, k + 1, 1 + p, 4:4 + span, :]
+                    part = y[s * span:(s + 1) * span, p * LANES:(p + 1) * LANES]
+                    value = inside((part + both) * 0.5 + bias1, sides1, k < 1, k >= groups1 - 1)
+                    put(sym, (e + 2 * p,), k, value, span)
+        return finish
+
     groups2 = tr // 8
-
     bias2 = column_ref[...]
-    def third(lo, hi):
-        spots = [(g, e) for g in range(lo, hi) for e in range(4)]
+
+    def third(g):
         cells = []
-        for g, e in spots:
+        for e in range(4):
             line = []
             for t in range(3):
                 for b in range(3):
@@ -214,15 +227,32 @@
             for p in range(2):
                 line.append(sym[e, g + 1, 1 + p, 4:4 + tc, :].astype(bf16))
             cells.append(jnp.concatenate(line, axis=1))
-        y = lax.dot_general(packed[0:2 * ch, LAST:PACKED], jnp.concatenate(cells, axis=0), NT, preferred_element_type=f32)
-        for s, (g, e) in enumerate(spots):
-            for p in range(2):
-                part = y[p * ch:(p + 1) * ch, s * tc:(s + 1) * tc]
-                acc[pl.ds(8 * g + e + 4 * p, ch, stride=tr), :] = part + bias2
-
-    for lo, hi in cuts(groups2, STEP2):
-        stage(functools.partial(third, lo, hi))
-    out_ref[...] = acc[...].reshape(ch, tr, tc).astype(out_ref.dtype)
+        y = lax.dot_general(packed[0:2 * ch, LAST:PACKED], jnp.concatenate(cells, axis=0), NT,
+                            preferred_element_type=f32)
+
+        def finish():
+            for e in range(4):
+                for p in range(2):
+                    part = y[p * ch:(p + 1) * ch, e * tc:(e + 1) * tc]
+                    acc[g, pl.ds(e + 4 * p, ch, stride=8), :] = part + bias2
+            out_ref[:, 8 * g:8 * g + 8, :] = acc[g].reshape(ch, 8, tc).astype(out_ref.dtype)
+        return finish
+
+    def together(makers):
+        def body():
+            for finish in [make() for make in makers]:
+                finish()
+        stage(body)
+
+    ready = 0
+    for lo, hi in cuts(groups1, STEP1):
+        makers = [functools.partial(second, lo, hi)]
+        if BESIDE and ready < groups2 and 2 * ready + 4 <= lo and (lo + ready) % 2:
+            makers.append(functools.partial(third, ready))
+            ready += 1
+        together(makers)
+    for g in range(ready, groups2):
+        together([functools.partial(third, g)])
 
 
 def filters(w, bias):
@@ -262,7 +292,7 @@
         ((2, tall, LANES), f32),
         ((2, 2, pairs0 // 2 + 1, 3, wide, LANES), f32),
         ((4, groups1 // 2 + 1, 3, span, LANES), f32),
-        ((ch * tr, LANES), f32),
+        ((tr // 8, ch * 8, LANES), f32),
     )
     return pl.pallas_call(
         functools.partial(decoder_kernel, tr, tc),

time: 25.3 us -> 25.7 us (1.016)
  Pallas kernels: 10.4 us -> 10.8 us
    pallas_call x1, Pallas kernels: 7.57 us -> 7.98 us  [decode(): pl.pallas_call(functools.partial(decoder_kernel, tr, tc), out_shape=jax.S...]
where the time goes in v7:
time: 25.7 us; the launch traced here: 25.5 us
  Pallas kernels  10.8 us (42%)
  starting transfers between devices  7.33 us (29%)
  waiting for transfers between devices  5.57 us (22%)
  local copies, waits for them, and re-layouts  1.77 us (7%)
    pallas_call x1, Pallas kernels, decode(): pl.pallas_call(functools.partial(decoder_kernel, tr, tc), out_shape=jax.S...  7.98 us
    all_to_all x1, starting transfers between devices, shards(): terms = lax.all_to_all(send, ('row', 'col'), 0, 0, tiled=True)  7.33 us
    all_to_all x1, waiting for transfers between devices, shards(): terms = lax.all_to_all(send, ('row', 'col'), 0, 0, tiled=True)  5.57 us
    pallas_call x1, Pallas kernels, project(): pl.pallas_call(project_kernel, out_shape=jax.ShapeDtypeStruct((peers, 3,...  2.08 us
    unnamed x4, local copies, waits for them, and re-layouts  1.77 us
    pallas_call x1, Pallas kernels, filters(): pl.pallas_call(filters_kernel, out_shape=[jax.ShapeDtypeStruct(*s) for s...  0.73 us
  transfers between devices with their start and end apart: 1, of which 1 were waited for; matrix products, arithmetic and copies ran while one was open for 0% of the time, Pallas kernels for 3%

profile of v7, /device:TPU:0, one launch (start us, length us, event | category | flops | bytes accessed | tf_op | source)
XLA Modules:
  0.0 25.5 jit_solution(1900185723478202695)
XLA Ops:
  0.0 2.1 %shard_map.55 = bf16[32,3,4,128]{3,2,1,0:T(4,128)(2,1)} custom-call(bf16[8,1536]{1,0:T(8,128)(2,1)} %bins_hbm.1, bf16[96,1536]{1,0:T(8,128)(2,1)} %row_hbm.1, bf16[96,1536]{1,0:T(8,128)(2,1)} %col_hbm.1), custom_call_target="tpu_custom_call" | custom-call | tf_op jit(solution)/shard_map/pallas_call | solution.py:330
  2.1 7.3 %all-to-all-start = ((bf16[32,3,4,128]{3,2,1,0:T(4,128)(2,1)}), bf16[32,3,4,128]{3,2,1,0:T(4,128)(2,1)S(1)}, u32[]{:S(2)}, u32[]{:S(2)}) async-start(bf16[32,3,4,128]{3,2,1,0:T(4,128)(2,1)} %shard_map.55), calls=%async_computation | async-start | bytes 196608 | tf_op jit(solution)/shard_map/all_to_all | solution.py:356
  9.4 0.0 copy-start
  9.4 1.1 %copy-done = bf16[3,9,96,96]{3,2,1,0:T(8,128)(2,1)S(1)} copy-done((bf16[3,9,96,96]{3,2,1,0:T(8,128)(2,1)S(1)}, bf16[3,9,96,96]{3,2,1,0:T(8,128)(2,1)}, u32[]{:S(2)}) %copy-start) | copy-done | bytes 497688
  10.5 0.0 copy-start.1
  10.5 0.7 %copy-done.1 = f32[3,96]{1,0:T(4,128)S(1)} copy-done((f32[3,96]{1,0:T(4,128)S(1)}, f32[3,96]{1,0:T(4,128)}, u32[]{:S(2)}) %copy-start.1) | copy-done | bytes 1176
  11.2 0.7 %shard_map.56 = (bf16[256,6016]{1,0:T(8,128)(2,1)S(1)}, f32[3,128]{1,0:T(4,128)S(1)}, f32[96,128]{1,0:T(8,128)S(1)}) custom-call(bf16[3,9,96,96]{3,2,1,0:T(8,128)(2,1)S(1)} %copy-done, f32[3,96]{1,0:T(4,128)S(1)} %copy-done.1), custom_call_target="tpu_custom_call" | custom-call | bytes 8388608 | tf_op jit(solution)/shard_map/pallas_call | solution.py:267
  11.9 5.6 %all-to-all-done.terms_ref = bf16[32,3,4,128]{3,2,1,0:T(4,128)(2,1)S(1)} async-done(((bf16[32,3,4,128]{3,2,1,0:T(4,128)(2,1)}), bf16[32,3,4,128]{3,2,1,0:T(4,128)(2,1)S(1)}, u32[]{:S(2)}, u32[]{:S(2)}) %all-to-all-start) | async-done | bytes 98336 | tf_op jit(solution)/shard_map/all_to_all | solution.py:356
  17.5 8.0 %shard_map.57 = bf16[96,16,128]{2,1,0:T(8,128)(2,1)} custom-call(bf16[32,3,4,128]{3,2,1,0:T(4,128)(2,1)S(1)} %all-to-all-done.terms_ref, bf16[256,6016]{1,0:T(8,128)(2,1)S(1)} %get-tuple-element.8.packed, f32[3,128]{1,0:T(4,128)S(1)} %get-tuple-element.9.bias_ref, f32[96,128]{1,0:T(8,128)S(1)} %get-tuple-element.10.column_ref), custom_call_target="tpu_custom_call" | custom-call | tf_op jit(solution)/shard_map/pallas_call | solution.py:297
Async XLA Ops:
  2.1 15.4 %all-to-all-start = ((bf16[32,3,4,128]{3,2,1,0:T(4,128)(2,1)}), bf16[32,3,4,128]{3,2,1,0:T(4,128)(2,1)S(1)}, u32[]{:S(2)}, u32[]{:S(2)}) async-start(bf16[32,3,4,128]{3,2,1,0:T(4,128)(2,1)} %shard_map.55), calls=%async_computation | async-start | bytes 196608 | tf_op jit(solution)/shard_map/all_to_all | solution.py:356
  9.4 1.1 %copy-start = (bf16[3,9,96,96]{3,2,1,0:T(8,128)(2,1)S(1)}, bf16[3,9,96,96]{3,2,1,0:T(8,128)(2,1)}, u32[]{:S(2)}) copy-start(bf16[3,9,96,96]{3,2,1,0:T(8,128)(2,1)} %w_ref.1) | copy-start | bytes 1492996
  10.5 0.7 %copy-start.1 = (f32[3,96]{1,0:T(4,128)S(1)}, f32[3,96]{1,0:T(4,128)}, u32[]{:S(2)}) copy-start(f32[3,96]{1,0:T(4,128)} %b_ref.1) | copy-start | bytes 3460
